TPU v7x, 32 devices: a whole 2x2x4 slice. The times are simulated.
32 devices in a mesh: parts: 2 (over x), ctx: 16 (over z, y, core).
Axes of the slice: x: 2, y: 2, z: 4, core: 2. Of those that a mesh axis runs over, the one named last changes fastest.
Arguments:
- queries: bfloat16 [256, 8192], P(('parts', 'ctx')), parts along dimension 0, may hold values from -24 to 24
- steer_ids: int32 [256], P(('parts', 'ctx')), parts along dimension 0, may hold values from 0 to 15
- steer_table: bfloat16 [16, 8192], replicated, may hold values from -3 to 3
- kv: bfloat16 [2, 32768, 1024], P(None, ('parts', 'ctx')), parts along dimension 1, may hold values from -4 to 4
- blocks: int32 [4, 128], P('parts'), parts along dimension 0, may hold values from 0 to 255, as said below
- w_out: bfloat16 [8192, 8192], P('ctx'), may hold values from -0.0625 to 0.0625
Outputs:
- projected: bfloat16 [256, 8192], P(('parts', 'ctx')), parts along dimension 0
There are 2 independent parts, one for each index of `parts`. A program takes and returns all parts, laid end to end along the dimension named above; an argument that names none is the same for every part. Nothing has to cross between parts.
Inputs may be any that keep to these rules, and one draw needn't show every extreme that they name: Each row lists 128 distinct key blocks and always includes block 0 and block 255.
All inputs are finite; a program needn't handle non-finite values.
Results may differ from a plain program's by a relative error of at most 0.0066.
Values may be sent and summed in bfloat16 or wider, within the bound.
No kernel may reach another device: no remote copies, remote signals or barrier semaphores. Data moves between devices by JAX's collectives and lax.ppermute only.
A program may use at most 64 MiB of HBM per device.

v0:
```python
import jax
import jax.numpy as jnp
from jax import lax
from jax.sharding import PartitionSpec as P

HEADS = 64
KV_HEADS = 8
HEAD = 128
D = 8192
BLOCK = 64


def apply_steer(queries, steer_ids, steer_table):
    lookup_ids = jnp.arange(steer_table.shape[0], dtype=jnp.int32)
    one_hot = (steer_ids[:, None] == lookup_ids[None, :]).astype(jnp.bfloat16)
    lookup = jnp.dot(one_hot, steer_table, preferred_element_type=jnp.float32)
    return (queries.astype(jnp.float32) + lookup).astype(jnp.bfloat16)


def local_keep(blocks, first_block, block_count, query_count):
    block_ids = first_block + jnp.arange(block_count, dtype=jnp.int32)
    hits = jnp.any(blocks[:, :, None] == block_ids[None, None, :], axis=1)
    full = jnp.broadcast_to(
        hits[:, None, :, None], (query_count // BLOCK, BLOCK, block_count, BLOCK)
    )
    return full.reshape(query_count, block_count * BLOCK)


def group_attend(q_rows, k_rows, v_rows, keep_rows):
    scores = lax.dot_general(
        q_rows, k_rows, (((1,), (1,)), ((), ())), preferred_element_type=jnp.float32
    )
    scores = scores * HEAD ** (-0.5)
    masked = jnp.where(keep_rows, scores, jnp.float32(-1e30))
    row_peak = jnp.max(masked, axis=1)
    weights = jnp.where(keep_rows, jnp.exp(masked - row_peak[:, None]), jnp.float32(0.0))
    row_total = jnp.sum(weights, axis=1)
    probs = weights.astype(jnp.bfloat16)
    partial_out = jnp.dot(probs, v_rows, preferred_element_type=jnp.float32)
    return (row_peak, row_total, partial_out)


def partial_attention(steered, kv_piece, keep_mask):
    query_count = steered.shape[0]
    ctx_count = kv_piece.shape[1]
    group_size = HEADS // KV_HEADS
    q_groups = steered.reshape(query_count, KV_HEADS, group_size, HEAD).transpose(1, 2, 0, 3)
    q_groups = q_groups.reshape(KV_HEADS, group_size * query_count, HEAD)
    k_groups = kv_piece[0].reshape(ctx_count, KV_HEADS, HEAD).transpose(1, 0, 2)
    v_groups = kv_piece[1].reshape(ctx_count, KV_HEADS, HEAD).transpose(1, 0, 2)
    keep_rows = jnp.tile(keep_mask, (group_size, 1))

    def one_group(triple):
        return group_attend(triple[0], triple[1], triple[2], keep_rows)

    peaks, totals, outs = lax.map(one_group, (q_groups, k_groups, v_groups))
    peaks = (
        peaks.reshape(KV_HEADS, group_size, query_count)
        .transpose(2, 0, 1)
        .reshape(query_count, HEADS)
    )
    totals = (
        totals.reshape(KV_HEADS, group_size, query_count)
        .transpose(2, 0, 1)
        .reshape(query_count, HEADS)
    )
    outs = (
        outs.reshape(KV_HEADS, group_size, query_count, HEAD)
        .transpose(2, 0, 1, 3)
        .reshape(query_count, HEADS * HEAD)
    )
    return (peaks, totals, outs)


def per_device(queries, steer_ids, steer_table, kv, blocks, w_out):
    steered_local = apply_steer(queries, steer_ids, steer_table)
    steered = lax.all_gather(steered_local, "ctx", axis=0, tiled=True)
    shard_count = lax.axis_size("ctx")
    my_index = lax.axis_index("ctx")
    query_count = steered.shape[0]
    block_count = kv.shape[1] // BLOCK
    keep_mask = local_keep(blocks, my_index * block_count, block_count, query_count)
    peaks, totals, outs = partial_attention(steered, kv, keep_mask)
    stat_width = max(HEADS, shard_count)
    per_entry = D // stat_width
    col_count = D // shard_count

    def spread(values):
        return jnp.repeat(values, stat_width // HEADS, axis=1)

    got_num, got_max, got_den = (
        lax.all_to_all(outs, "ctx", split_axis=1, concat_axis=0, tiled=True),
        lax.all_to_all(spread(peaks), "ctx", split_axis=1, concat_axis=0, tiled=True),
        lax.all_to_all(spread(totals), "ctx", split_axis=1, concat_axis=0, tiled=True),
    )
    got_num = got_num.reshape(shard_count, query_count, col_count)
    got_max = got_max.reshape(shard_count, query_count, stat_width // shard_count)
    got_den = got_den.reshape(shard_count, query_count, stat_width // shard_count)
    overall = jnp.max(got_max, axis=0)
    scales = jnp.exp(got_max - overall[None])
    denominator = jnp.sum(scales * got_den, axis=0)
    numerator = jnp.sum(jnp.repeat(scales, per_entry, axis=2) * got_num, axis=0)
    attended = (numerator / jnp.repeat(denominator, per_entry, axis=1)).astype(jnp.bfloat16)
    return lax.psum_scatter(
        jnp.dot(attended, w_out, preferred_element_type=jnp.float32),
        "ctx",
        scatter_dimension=0,
        tiled=True,
    ).astype(jnp.bfloat16)


def solution(mesh):
    return jax.shard_map(
        per_device,
        mesh=mesh,
        in_specs=(
            P(("parts", "ctx"), None),
            P(("parts", "ctx")),
            P(),
            P(None, ("parts", "ctx"), None),
            P("parts", None),
            P("ctx", None),
        ),
        out_specs=P(("parts", "ctx"), None),
        check_vma=False,
    )
```

profile of v0, /device:TPU:0, one launch (start us, length us, event | category | flops | bytes accessed | tf_op | source)
XLA Modules:
  0.0 324.4 jit_solution(4779056116548888666)
XLA Ops:
  9.3 4.0 %fusion.32 = (bf16[1,1024,1024]{2,1,0:T(8,128)(2,1)S(1)}, bf16[1,1024,1024]{2,1,0:T(8,128)(2,1)}) fusion(bf16[2,1024,1024]{2,1,0:T(8,128)(2,1)} %param.11), kind=kLoop, calls=%fused_computation.38 | loop fusion | bytes 8388608 | tf_op jit(solution)/shard_map/slice | solution.py:50
  13.4 4.0 %copy.38 = bf16[1,1024,1024]{1,2,0:T(8,128)(2,1)} copy(bf16[1,1024,1024]{2,1,0:T(8,128)(2,1)} %get-tuple-element.124) | data formatting | bytes 4194304
  17.3 2.6 copy.39
  20.9 32.8 %all-gather.2.cloned.1.call-done = bf16[128,8192]{1,0:T(8,128)(2,1)} async-done(((bf16[8,8192]{1,0:T(8,128)(2,1)}), bf16[128,8192]{1,0:T(8,128)(2,1)}) %all-gather.2.cloned.1.call-update) | async-done | bytes 2097168 | tf_op jit(solution)/shard_map/all_gather | solution.py:77
  53.7 2.2 copy.41
  57.3 58.5 %while.15 = (s32[]{:T(128)}, f32[8,1024]{1,0:T(8,128)S(1)}, f32[8,1024]{1,0:T(8,128)S(1)}, f32[8,1024,128]{2,1,0:T(8,128)}, bf16[8,1024,128]{2,1,0:T(8,128)(2,1)...) while((s32[]{:T(128)}, f32[8,1024]{1,0:T(8,128)S(1)}, ...), condition=%wide.region_4.5_spmd.clone, body=%wide.region_1.4_spmd.clone.sunk | while | flops 550500352 | bytes 18253932 | solution.py:56
  59.8 3.2 fusion.46
  67.1 3.2 fusion.46
  74.4 3.2 fusion.46
  79.7 2.0 fusion.44
  81.7 3.2 fusion.46
  89.1 3.2 fusion.46
  96.4 3.2 fusion.46
  103.7 3.2 fusion.46
  111.0 3.2 fusion.46
  116.4 3.5 %all-to-all-start = ((f32[128,16,4]{0,2,1:T(4,128)}), f32[128,16,4]{0,2,1:T(4,128)S(1)}, u32[]{:S(2)}, u32[]{:S(2)}) async-start(f32[128,16,4]{0,2,1:T(4,128)} %bitcast.7), calls=%async_computation | async-start | bytes 65536 | tf_op jit(solution)/shard_map/all_to_all | solution.py:93
  120.5 6.0 %all-to-all-done = f32[128,16,4]{0,2,1:T(4,128)S(1)} async-done(((f32[128,16,4]{0,2,1:T(4,128)}), f32[128,16,4]{0,2,1:T(4,128)S(1)}, u32[]{:S(2)}, u32[]{:S(2)}) %all-to-all-start) | async-done | bytes 32800 | tf_op jit(solution)/shard_map/all_to_all | solution.py:93
  126.5 3.5 %all-to-all-start.2 = ((f32[128,16,4]{0,2,1:T(4,128)}), f32[128,16,4]{0,2,1:T(4,128)S(1)}, u32[]{:S(2)}, u32[]{:S(2)}) async-start(f32[128,16,4]{0,2,1:T(4,128)} %bitcast.15), calls=%async_computation.2 | async-start | bytes 65536 | tf_op jit(solution)/shard_map/all_to_all | solution.py:94
  130.0 5.4 %copy.35 = f32[128,8,8,128]{0,3,2,1:T(8,128)} copy(f32[128,8,8,128]{3,0,2,1:T(8,128)} %bitcast.11) | data formatting | bytes 8388608 | tf_op jit(solution)/shard_map/transpose | solution.py:69
  136.6 4.8 %all-to-all-start.1 = ((f32[128,16,512]{0,2,1:T(8,128)}), f32[128,16,512]{0,2,1:T(8,128)}, u32[]{:S(2)}, u32[]{:S(2)}) async-start(f32[128,16,512]{0,2,1:T(8,128)} %bitcast.118), calls=%async_computation.1 | async-start | bytes 8388608 | tf_op jit(solution)/shard_map/all_to_all | solution.py:92
  141.5 77.4 %all-to-all-done.1 = f32[128,16,512]{0,2,1:T(8,128)} async-done(((f32[128,16,512]{0,2,1:T(8,128)}), f32[128,16,512]{0,2,1:T(8,128)}, u32[]{:S(2)}, u32[]{:S(2)}) %all-to-all-start.1) | async-done | bytes 4194336 | tf_op jit(solution)/shard_map/all_to_all | solution.py:92
  218.9 2.5 fusion.26
  221.4 6.6 %fusion.33 = f32[128,8192]{1,0:T(8,128)} fusion(bf16[128,512]{0,1:T(8,128)(2,1)S(1)} %fusion.27, bf16[512,8192]{1,0:T(8,128)(2,1)} %param.13), kind=kOutput, calls=%fused_computation.39 | convolution fusion | flops 1073741824 | bytes 12713984 | tf_op jit(solution)/shard_map/dot_general | solution.py:105
  228.1 87.8 %reduce-scatter.2.cloned.1.call-done = f32[8,8192]{1,0:T(8,128)} async-done(((f32[128,8192]{1,0:T(8,128)}), f32[8,8192]{1,0:T(8,128)}) %reduce-scatter.2.cloned.1.call-update) | async-done | bytes 262160 | tf_op jit(solution)/shard_map/reduce_scatter | solution.py:104
  (64 shorter events, 39.6 us)
Async XLA Ops:
  6.5 1.0 copy-start
  6.5 47.2 %all-gather.2.cloned.1.call-start = ((), (), s32[]{:S(2)}) async-start(), calls=%async_computation.4 | async-start | bytes 2228224 | tf_op jit(solution)/shard_map/all_gather | solution.py:77
  13.4 6.5 %copy-start.1 = (s32[2,128]{1,0:T(2,128)S(1)}, s32[2,128]{1,0:T(2,128)}, u32[]{:S(2)}) copy-start(s32[2,128]{1,0:T(2,128)} %param.12) | copy-start | bytes 3076
  116.4 10.1 %all-to-all-start = ((f32[128,16,4]{0,2,1:T(4,128)}), f32[128,16,4]{0,2,1:T(4,128)S(1)}, u32[]{:S(2)}, u32[]{:S(2)}) async-start(f32[128,16,4]{0,2,1:T(4,128)} %bitcast.7), calls=%async_computation | async-start | bytes 65536 | tf_op jit(solution)/shard_map/all_to_all | solution.py:93
  126.5 10.1 %all-to-all-start.2 = ((f32[128,16,4]{0,2,1:T(4,128)}), f32[128,16,4]{0,2,1:T(4,128)S(1)}, u32[]{:S(2)}, u32[]{:S(2)}) async-start(f32[128,16,4]{0,2,1:T(4,128)} %bitcast.15), calls=%async_computation.2 | async-start | bytes 65536 | tf_op jit(solution)/shard_map/all_to_all | solution.py:94
  136.6 82.3 %all-to-all-start.1 = ((f32[128,16,512]{0,2,1:T(8,128)}), f32[128,16,512]{0,2,1:T(8,128)}, u32[]{:S(2)}, u32[]{:S(2)}) async-start(f32[128,16,512]{0,2,1:T(8,128)} %bitcast.118), calls=%async_computation.1 | async-start | bytes 8388608 | tf_op jit(solution)/shard_map/all_to_all | solution.py:92
  141.3 174.6 %reduce-scatter.2.cloned.1.call-start = ((), (), s32[]{:S(2)}) async-start(), calls=%async_computation.5 | async-start | bytes 4456448 | tf_op jit(solution)/shard_map/reduce_scatter | solution.py:104
Sparse Core Ops, SparseCore 0:
  9.5 44.1 all-gather.1
  228.2 87.6 reduce-scatter.1
where the time goes:
time: 326 us; the launch traced here: 324 us
  waiting for transfers between devices  205 us (63%)
  matrix products  50.6 us (16%)
  local copies, waits for them, and re-layouts  28 us (9%)
  other arithmetic  14.8 us (5%)
  between operations  13.5 us (4%)
  starting transfers between devices  11.8 us (4%)
    reduce_scatter x1, waiting for transfers between devices, per_device(): lax.psum_scatter(jnp.dot(attended, w_out, preferred_element_type=jnp.floa...  87.8 us
    all_to_all x1, waiting for transfers between devices, per_device(): lax.all_to_all(outs, 'ctx', split_axis=1, concat_axis=0, tiled=True)  77.4 us
    all_gather x1, waiting for transfers between devices, per_device(): steered = lax.all_gather(steered_local, 'ctx', axis=0, tiled=True)  32.8 us
    dot_general x8, matrix products, group_attend(): partial_out = jnp.dot(probs, v_rows, preferred_element_type=jnp.float32)  25.8 us
    dot_general x8, matrix products, group_attend(): lax.dot_general(q_rows, k_rows, (((1,), (1,)), ((), ())), preferred_eleme...  16.4 us
    unnamed x10, local copies, waits for them, and re-layouts  11.2 us
    reduce_sum x8, other arithmetic, group_attend(): row_total = jnp.sum(weights, axis=1)  10.4 us
    dot_general x1, matrix products, per_device(): jnp.dot(attended, w_out, preferred_element_type=jnp.float32)  6.63 us
  transfers between devices with their start and end apart: 5, of which 5 were waited for; matrix products, arithmetic and copies ran while one was open for 5% of the time, Pallas kernels for 0%

commit v1 on v0

--- a/solution.py
+++ b/solution.py
@@ -1,6 +1,8 @@
 import jax
 import jax.numpy as jnp
 from jax import lax
+from jax.experimental import pallas as pl
+from jax.experimental.pallas import tpu as pltpu
 from jax.sharding import PartitionSpec as P
 
 HEADS = 64
@@ -109,9 +111,255 @@
     ).astype(jnp.bfloat16)
 
 
+NONE = -1e30
+LOG2E = 1.4426950408889634
+STAT_ROWS = 16
+
+
+def attend_kernel(heads, tile, order, *refs):
+    n_blocks = order.shape[0]
+    q_blocks = refs[:n_blocks]
+    k_own, k_far, v_own, v_far, keep, out, q_all, scores = refs[n_blocks:]
+    group = pl.program_id(0)
+    block_rows = q_blocks[0].shape[0]
+    rows = n_blocks * block_rows
+    ctx = k_own.shape[1]
+    per_tile = tile // BLOCK
+    to_log2 = HEAD ** (-0.5) * LOG2E
+
+    for at in range(n_blocks):
+        q_all[order[at]] = q_blocks[at][...]
+
+    pieces = [(k_own, v_own, 0, t) for t in range(ctx // tile)]
+    pieces += [(k_far, v_far, ctx // BLOCK, t) for t in range(ctx // tile)]
+    stats = [[], [], []]
+    for pair in range(heads // 2):
+        q_pair = jnp.concatenate(
+            [
+                q_all[:, :, (2 * pair + j) * HEAD : (2 * pair + j + 1) * HEAD].reshape(rows, HEAD)
+                for j in range(2)
+            ],
+            axis=0,
+        )
+        peak = jnp.full((1, 2 * rows), NONE, jnp.float32)
+        for at, (k_ref, v_ref, first, t) in enumerate(pieces):
+            piece = lax.dot_general(
+                k_ref[0, t * tile : (t + 1) * tile, :],
+                q_pair,
+                (((1,), (1,)), ((), ())),
+                preferred_element_type=jnp.float32,
+            )
+            scores[pair, at * tile : (at + 1) * tile, :] = piece
+            for b in range(per_tile):
+                kept = keep[pl.ds(first + t * per_tile + b, 1), :]
+                best = jnp.max(piece[b * BLOCK : (b + 1) * BLOCK, :], axis=0, keepdims=True)
+                peak = jnp.maximum(peak, jnp.where(kept > 0.0, best * to_log2, NONE))
+        peak_sent = peak.astype(jnp.bfloat16)
+        peak = peak_sent.astype(jnp.float32)
+        total = jnp.zeros((8, 2 * rows), jnp.float32)
+        value = jnp.zeros((HEAD, 2 * rows), jnp.float32)
+        for at, (k_ref, v_ref, first, t) in enumerate(pieces):
+            probs = []
+            for b in range(per_tile):
+                kept = keep[pl.ds(first + t * per_tile + b, 1), :]
+                shift = jnp.where(kept > 0.0, peak, -NONE)
+                low = at * tile + b * BLOCK
+                weights = jnp.exp2(scores[pair, low : low + BLOCK, :] * to_log2 - shift)
+                total = total + jnp.sum(weights.reshape(BLOCK // 8, 8, 2 * rows), axis=0)
+                probs.append(weights.astype(jnp.bfloat16))
+            value = value + jnp.dot(
+                v_ref[:, t * tile : (t + 1) * tile],
+                jnp.concatenate(probs, axis=0),
+                preferred_element_type=jnp.float32,
+            )
+        total = jnp.sum(total, axis=0, keepdims=True)
+        total_high = total.astype(jnp.bfloat16).astype(jnp.float32)
+        total_low = total - total_high
+        for j in range(2):
+            half = slice(j * rows, (j + 1) * rows)
+            low = (2 * pair + j) * HEAD
+            out[0, low : low + HEAD, :] = value[:, half].astype(jnp.bfloat16)
+            stats[0].append(peak[:, half])
+            stats[1].append(total_high[:, half])
+            stats[2].append(total_low[:, half])
+    flat = stats[0] + stats[1] + stats[2]
+    flat += [jnp.zeros_like(flat[0])] * (STAT_ROWS - len(flat))
+    out[0, heads * HEAD :, :] = jnp.concatenate(flat, axis=0).astype(jnp.bfloat16)
+
+
+def attend(q_blocks, order, kv, kv_far, v_turned, v_far_turned, keep, heads, tile=256):
+    block_rows = q_blocks[0].shape[0]
+    rows = block_rows * len(q_blocks)
+    ctx = kv.shape[1]
+    width = heads * HEAD
+    length = width + STAT_ROWS
+
+    def column(g, order_ref):
+        return (0, g)
+
+    return pl.pallas_call(
+        lambda *refs: attend_kernel(heads, tile, *refs),
+        grid_spec=pltpu.PrefetchScalarGridSpec(
+            num_scalar_prefetch=1,
+            grid=(KV_HEADS,),
+            in_specs=[pl.BlockSpec((block_rows, width), column) for _ in q_blocks]
+            + [
+                pl.BlockSpec((1, ctx, HEAD), lambda g, o: (0, 0, g)),
+                pl.BlockSpec((1, ctx, HEAD), lambda g, o: (0, 0, g)),
+                pl.BlockSpec((HEAD, ctx), lambda g, o: (g, 0)),
+                pl.BlockSpec((HEAD, ctx), lambda g, o: (g, 0)),
+                pl.BlockSpec(keep.shape, lambda g, o: (0, 0)),
+            ],
+            out_specs=pl.BlockSpec((1, length, rows), lambda g, o: (g, 0, 0)),
+            scratch_shapes=[
+                pltpu.VMEM((len(q_blocks), block_rows, width), jnp.bfloat16),
+                pltpu.VMEM((heads // 2, 2 * ctx, 2 * rows), jnp.float32),
+            ],
+        ),
+        out_shape=jax.ShapeDtypeStruct((KV_HEADS, length, rows), jnp.bfloat16),
+        compiler_params=pltpu.CompilerParams(
+            dimension_semantics=("arbitrary",), vmem_limit_bytes=40 * 1024 * 1024
+        ),
+        cost_estimate=pl.CostEstimate(
+            flops=4 * rows * KV_HEADS * width * 2 * ctx,
+            bytes_accessed=8 * ctx * KV_HEADS * HEAD,
+            transcendentals=rows * KV_HEADS * heads * 2 * ctx,
+        ),
+        name="attend",
+    )(order, *q_blocks, kv, kv_far, v_turned, v_far_turned, keep)
+
+
+def project_kernel(heads, core, parts, w_ref, kept, sent, attended):
+    @pl.when(pl.program_id(0) == 0)
+    def _():
+        stats = parts[:, heads * HEAD :, :].astype(jnp.float32)
+        peaks = stats[:, :heads, :]
+        totals = stats[:, heads : 2 * heads, :] + stats[:, 2 * heads : 3 * heads, :]
+        scales = jnp.exp2(peaks - jnp.max(peaks, axis=0, keepdims=True))
+        below = jnp.sum(scales * totals, axis=0)
+        for h in range(heads):
+            above = jnp.zeros((HEAD, parts.shape[2]), jnp.float32)
+            for s in range(parts.shape[0]):
+                piece = parts[s, h * HEAD : (h + 1) * HEAD, :].astype(jnp.float32)
+                above = above + piece * scales[s, h : h + 1, :]
+            mean = above / below[h : h + 1, :]
+            attended[:, h * HEAD : (h + 1) * HEAD] = mean.T.astype(jnp.bfloat16)
+
+    full = jnp.dot(attended[...], w_ref[...], preferred_element_type=jnp.float32)
+    per_dev, tile = kept.shape[1], kept.shape[2]
+    full = full.reshape(kept.shape[0], 2, per_dev, tile)
+    first = core[0] == 0
+    kept[...] = jnp.where(first, full[:, 0], full[:, 1])
+    away = jnp.where(first, full[:, 1], full[:, 0])
+    sent[...] = away.reshape(kept.shape[0] * per_dev, tile).astype(jnp.bfloat16)
+
+
+def project(parts, core, w_out, heads, per_dev, tile=1024):
+    shards, length, rows = parts.shape
+    chips = rows // (2 * per_dev)
+    return pl.pallas_call(
+        lambda *refs: project_kernel(heads, *refs),
+        grid_spec=pltpu.PrefetchScalarGridSpec(
+            num_scalar_prefetch=1,
+            grid=(D // tile,),
+            in_specs=[
+                pl.BlockSpec((shards, length, rows), lambda j, c: (0, 0, 0)),
+                pl.BlockSpec((heads * HEAD, tile), lambda j, c: (0, j)),
+            ],
+            out_specs=[
+                pl.BlockSpec((chips, per_dev, tile), lambda j, c: (0, 0, j)),
+                pl.BlockSpec((chips * per_dev, tile), lambda j, c: (0, j)),
+            ],
+            scratch_shapes=[pltpu.VMEM((rows, heads * HEAD), jnp.bfloat16)],
+        ),
+        out_shape=[
+            jax.ShapeDtypeStruct((chips, per_dev, D), jnp.float32),
+            jax.ShapeDtypeStruct((chips * per_dev, D), jnp.bfloat16),
+        ],
+        compiler_params=pltpu.CompilerParams(dimension_semantics=("arbitrary",)),
+        cost_estimate=pl.CostEstimate(
+            flops=2 * rows * heads * HEAD * D, bytes_accessed=3 * heads * HEAD * D, transcendentals=0
+        ),
+        name="project",
+    )(core, parts, w_out)
+
+
+def ring_of(chips):
+    return [c for c in range(0, chips, 2)] + [c for c in range(chips - 1, 0, -2)]
+
+
+def paired_device(queries, steer_ids, steer_table, kv, blocks, w_out):
+    n = lax.axis_size("ctx")
+    me = lax.axis_index("ctx")
+    chips = n // 2
+    core = me % 2
+    chip = me // 2
+    per_dev = queries.shape[0]
+    rows = per_dev * n
+    width = D // n
+    heads = width // HEAD
+    swap = [(i, i ^ 1) for i in range(n)]
+    evens_odds = [[2 * c for c in range(chips)], [2 * c + 1 for c in range(chips)]]
+    ring = ring_of(chips)
+
+    steered = apply_steer(queries, steer_ids, steer_table)
+    halves = steered.reshape(per_dev, chips, 2, width)
+    mine = jnp.where(core == 0, halves[:, :, 0], halves[:, :, 1]).reshape(per_dev, D // 2)
+    other = jnp.where(core == 0, halves[:, :, 1], halves[:, :, 0]).reshape(per_dev, D // 2)
+    theirs = lax.ppermute(other, "ctx", swap)
+    block = jnp.concatenate(
+        [jnp.where(core == 0, mine, theirs), jnp.where(core == 0, theirs, mine)], axis=0
+    )
+    kv_far = lax.ppermute(kv, "ctx", swap)
+
+    def hop(step):
+        return [
+            (2 * ring[p] + c, 2 * ring[(p + step) % chips] + c) for p in range(chips) for c in range(2)
+        ]
+
+    found, offsets = [block], [0]
+    ahead, behind = block, block
+    for s in range(1, chips // 2 + 1):
+        ahead = lax.ppermute(ahead, "ctx", hop(1))
+        found.append(ahead)
+        offsets.append(-s)
+        if s < chips - s:
+            behind = lax.ppermute(behind, "ctx", hop(-1))
+            found.append(behind)
+            offsets.append(s)
+    ring_array = jnp.array(ring, jnp.int32)
+    place_array = jnp.array([ring.index(c) for c in range(chips)], jnp.int32)
+    place = place_array[chip]
+    order = ring_array[(place + jnp.array(offsets, jnp.int32)) % chips]
+
+    v_turned = kv[1].T
+    v_far_turned = kv_far[1].T
+    block_count = kv.shape[1] // BLOCK
+    ids = jnp.arange(block_count, dtype=jnp.int32)
+    ids = jnp.concatenate([me * block_count + ids, (me ^ 1) * block_count + ids])
+    hits = jnp.any(blocks[:, None, :] == ids[None, :, None], axis=2)
+    keep = jnp.repeat(hits.T.astype(jnp.float32), BLOCK, axis=1)
+    keep = jnp.concatenate([keep, keep], axis=1)
+
+    message = attend(found, order, kv, kv_far, v_turned, v_far_turned, keep, heads)
+    parts = lax.all_to_all(
+        message, "ctx", split_axis=0, concat_axis=0, axis_index_groups=evens_odds, tiled=True
+    )
+    kept, sent = project(parts, core.reshape(1), w_out, heads, per_dev)
+    got = lax.ppermute(sent, "ctx", swap)
+    summed = (kept.reshape(chips * per_dev, D) + got.astype(jnp.float32)).astype(jnp.bfloat16)
+    pieces = lax.all_to_all(
+        summed, "ctx", split_axis=0, concat_axis=0, axis_index_groups=evens_odds, tiled=True
+    )
+    pieces = pieces.reshape(chips, per_dev, D).astype(jnp.float32)
+    return jnp.sum(pieces, axis=0).astype(jnp.bfloat16)
+
+
 def solution(mesh):
+    n = mesh.shape["ctx"]
+    paired = n == 2 * KV_HEADS
     return jax.shard_map(
-        per_device,
+        paired_device if paired else per_device,
         mesh=mesh,
         in_specs=(
             P(("parts", "ctx"), None),

time: 326 us -> 140 us (0.43)
  waiting for transfers between devices: 205 us -> 14.9 us
  blocking collectives: 0 us -> 57.5 us
  matrix products: 50.6 us -> 0.23 us
  Pallas kernels: 0 us -> 30.8 us
  between operations: 13.5 us -> 0.14 us
  other arithmetic: 14.8 us -> 3.57 us
  local copies, waits for them, and re-layouts: 28 us -> 22.8 us
    reduce_scatter x1 -> x0, waiting for transfers between devices: 87.8 us -> none  [per_device(): lax.psum_scatter(jnp.dot(attended, w_out, preferred_element_type=jnp.floa...]
    all_to_all x3 -> x0, waiting for transfers between devices: 84.6 us -> none  [the longest x1 77.4 us: per_device(): lax.all_to_all(outs, 'ctx', split_axis=1, concat_axis=0, tiled=True)]
    all_to_all x0 -> x2, blocking collectives: none -> 57.5 us  [the longest x1 28.7 us: paired_device(): lax.all_to_all(message, 'ctx', split_axis=0, concat_axis=0, axis_index_gr...]
    dot_general x17 -> x0, matrix products: 48.8 us -> none  [the longest x8 25.8 us: group_attend(): partial_out = jnp.dot(probs, v_rows, preferred_element_type=jnp.float32)]
    all_gather x1 -> x0, waiting for transfers between devices: 32.8 us -> none  [per_device(): steered = lax.all_gather(steered_local, 'ctx', axis=0, tiled=True)]
    pallas_call x0 -> x2, Pallas kernels: none -> 30.8 us  [the longest x1 21.9 us: attend(): pl.pallas_call(lambda *refs: attend_kernel(heads, tile, *refs), grid_spec...]
    ppermute x0 -> x10, waiting for transfers between devices: none -> 14.9 us  [the longest x4 7.91 us: paired_device(): ahead = lax.ppermute(ahead, 'ctx', hop(1))]
    reduce_sum x10 -> x1, other arithmetic: 13 us -> 0.81 us  [paired_device(): return jnp.sum(pieces, axis=0).astype(jnp.bfloat16)]
  transfers between devices with their start and end apart: 5 -> 10, of which waited for: 5 -> 5; matrix products, arithmetic and copies ran while one was open for 5% -> 10% of each run, Pallas kernels for 0% -> 0%
where the time goes in v1:
time: 140 us
  blocking collectives  57.5 us (41%)
  Pallas kernels  30.8 us (22%)
  local copies, waits for them, and re-layouts  22.8 us (16%)
  waiting for transfers between devices  14.9 us (11%)
  starting transfers between devices  9.66 us (7%)
  other arithmetic  3.57 us (3%)
    all_to_all x1, blocking collectives, paired_device(): lax.all_to_all(message, 'ctx', split_axis=0, concat_axis=0, axis_index_gr...  28.7 us
    all_to_all x1, blocking collectives, paired_device(): lax.all_to_all(summed, 'ctx', split_axis=0, concat_axis=0, axis_index_gro...  28.7 us
    pallas_call x1, Pallas kernels, attend(): pl.pallas_call(lambda *refs: attend_kernel(heads, tile, *refs), grid_spec...  21.9 us
    unnamed x19, local copies, waits for them, and re-layouts  10.1 us
    pallas_call x1, Pallas kernels, project(): pl.pallas_call(lambda *refs: project_kernel(heads, *refs), grid_spec=pltp...  8.95 us
    ppermute x4, starting transfers between devices, paired_device(): ahead = lax.ppermute(ahead, 'ctx', hop(1))  8.5 us
    ppermute x4, waiting for transfers between devices, paired_device(): ahead = lax.ppermute(ahead, 'ctx', hop(1))  7.91 us
    ppermute x1, local copies, waits for them, and re-layouts, paired_device(): kv_far = lax.ppermute(kv, 'ctx', swap)  6.25 us
  transfers between devices with their start and end apart: 10, of which 5 were waited for; matrix products, arithmetic and copies ran while one was open for 10% of the time, Pallas kernels for 0%

profile of v1, /device:TPU:0, one launch (start us, length us, event | category | flops | bytes accessed | tf_op | source)
XLA Modules:
  0.0 139.6 jit_solution(12060064727955056054)
XLA Ops:
  0.0 6.3 %copy.22 = bf16[2,1024,1024]{1,2,0:T(8,128)(2,1)} copy(bf16[2,1024,1024]{2,1,0:T(8,128)(2,1)} %refs_9_.1) | data formatting | bytes 8388608 | tf_op args[3]
  7.2 0.6 dynamic_slice.3
  7.9 1.8 %slice_bitcast_fusion.1.refs_11_ = bf16[1024,1024]{1,0:T(8,128)(2,1)S(1)} fusion(bf16[2,1024,1024]{1,2,0:T(8,128)(2,1)} %copy.22), kind=kLoop, calls=%fused_computation.4 | loop fusion | bytes 4194304 | tf_op jit(solution)/shard_map/transpose | solution.py:335
  9.9 4.1 %collective-permute-done = bf16[8,4096]{1,0:T(8,128)(2,1)S(1)} collective-permute-done((bf16[8,4096]{1,0:T(8,128)(2,1)S(1)}, bf16[8,4096]{1,0:T(8,128)(2,1)S(1)}, u32[]{:S(2)}, u32[]{:S(2)}) %collective-permute-start) | collective-permute-done | bytes 65568 | tf_op jit(solution)/shard_map/ppermute | solution.py:309
  14.0 3.0 %collective-permute-start.1 = (bf16[16,4096]{1,0:T(8,128)(2,1)S(1)}, bf16[16,4096]{1,0:T(8,128)(2,1)S(1)}, u32[]{:S(2)}, u32[]{:S(2)}) collective-permute-start(bf16[16,4096]{1,0:T(8,128)(2,1)S(1)} %pad_maximum_fusion.refs_1_), channel_id=1, source_target_pairs={{0,4},{1,5},{4,8},{5,9},{8,12},{9,13},{12,14},{13,15},{14,10},{15,... | collective-permute-start | bytes 393224 | tf_op jit(solution)/shard_map/ppermute | solution.py:323
  17.0 3.7 %collective-permute-done.1.refs_2_ = bf16[16,4096]{1,0:T(8,128)(2,1)S(1)} collective-permute-done((bf16[16,4096]{1,0:T(8,128)(2,1)S(1)}, bf16[16,4096]{1,0:T(8,128)(2,1)S(1)}, u32[]{:S(2)}, u32[]{:S(2)}) %collective-permute-start.1) | collective-permute-done | bytes 131104 | tf_op jit(solution)/shard_map/ppermute | solution.py:323
  20.7 1.8 %collective-permute-start.3 = (bf16[16,4096]{1,0:T(8,128)(2,1)S(1)}, bf16[16,4096]{1,0:T(8,128)(2,1)S(1)}, u32[]{:S(2)}, u32[]{:S(2)}) collective-permute-start(bf16[16,4096]{1,0:T(8,128)(2,1)S(1)} %collective-permute-done.1.refs_2_), channel_id=1, source_target_pairs={{0,4},{1,5},{4,8},{5,9},{8,12},{9,13},{12,14},{13,15},{14,10},{15,... | collective-permute-start | bytes 393224 | tf_op jit(solution)/shard_map/ppermute | solution.py:323
  22.5 0.6 compare_select_fusion
  23.4 2.2 %collective-permute-done.3.refs_4_ = bf16[16,4096]{1,0:T(8,128)(2,1)S(1)} collective-permute-done((bf16[16,4096]{1,0:T(8,128)(2,1)S(1)}, bf16[16,4096]{1,0:T(8,128)(2,1)S(1)}, u32[]{:S(2)}, u32[]{:S(2)}) %collective-permute-start.3) | collective-permute-done | bytes 131104 | tf_op jit(solution)/shard_map/ppermute | solution.py:323
  25.7 1.8 %collective-permute-start.5 = (bf16[16,4096]{1,0:T(8,128)(2,1)S(1)}, bf16[16,4096]{1,0:T(8,128)(2,1)S(1)}, u32[]{:S(2)}, u32[]{:S(2)}) collective-permute-start(bf16[16,4096]{1,0:T(8,128)(2,1)S(1)} %collective-permute-done.3.refs_4_), channel_id=1, source_target_pairs={{0,4},{1,5},{4,8},{5,9},{8,12},{9,13},{12,14},{13,15},{14,10},{15,... | collective-permute-start | bytes 393224 | tf_op jit(solution)/shard_map/ppermute | solution.py:323
  27.8 0.6 gather_fusion
  28.7 1.9 %collective-permute-done.5.refs_6_ = bf16[16,4096]{1,0:T(8,128)(2,1)S(1)} collective-permute-done((bf16[16,4096]{1,0:T(8,128)(2,1)S(1)}, bf16[16,4096]{1,0:T(8,128)(2,1)S(1)}, u32[]{:S(2)}, u32[]{:S(2)}) %collective-permute-start.5) | collective-permute-done | bytes 131104 | tf_op jit(solution)/shard_map/ppermute | solution.py:323
  30.6 1.9 %collective-permute-start.7 = (bf16[16,4096]{1,0:T(8,128)(2,1)S(1)}, bf16[16,4096]{1,0:T(8,128)(2,1)S(1)}, u32[]{:S(2)}, u32[]{:S(2)}) collective-permute-start(bf16[16,4096]{1,0:T(8,128)(2,1)S(1)} %collective-permute-done.5.refs_6_), channel_id=1, source_target_pairs={{0,4},{1,5},{4,8},{5,9},{8,12},{9,13},{12,14},{13,15},{14,10},{15,... | collective-permute-start | bytes 393224 | tf_op jit(solution)/shard_map/ppermute | solution.py:323
  32.6 3.1 %slice_bitcast_fusion.refs_12_ = bf16[1024,1024]{1,0:T(8,128)(2,1)} fusion(bf16[2,1024,1024]{1,2,0:T(8,128)(2,1)} %collective-permute-done.8), kind=kLoop, calls=%fused_computation.3 | loop fusion | bytes 4194304 | tf_op jit(solution)/shard_map/transpose | solution.py:336
  35.7 6.2 %copy.25.refs_10_ = bf16[2,1024,1024]{2,1,0:T(8,128)(2,1)} copy(bf16[2,1024,1024]{1,2,0:T(8,128)(2,1)} %collective-permute-done.8) | data formatting | bytes 8388608 | tf_op jit(solution)/shard_map/ppermute | solution.py:313
  42.0 2.2 %copy-done.1 = bf16[2,1024,1024]{2,1,0:T(8,128)(2,1)S(1)} copy-done((bf16[2,1024,1024]{2,1,0:T(8,128)(2,1)S(1)}, bf16[2,1024,1024]{2,1,0:T(8,128)(2,1)}, u32[]{:S(2)}) %copy-start.1) | copy-done | bytes 4194328
  44.2 1.6 %copy-done.2 = bf16[1024,1024]{1,0:T(8,128)(2,1)S(1)} copy-done((bf16[1024,1024]{1,0:T(8,128)(2,1)S(1)}, bf16[1024,1024]{1,0:T(8,128)(2,1)}, u32[]{:S(2)}) %copy-start.2) | copy-done | bytes 2097176
  45.8 21.9 %attend.1 = bf16[8,528,128]{2,1,0:T(8,128)(2,1)S(1)} custom-call(s32[8]{0:T(128)S(1)} %gather_fusion, bf16[16,4096]{1,0:T(8,128)(2,1)S(1)} %pad_maximum_fusion.refs_1_, bf16[16,4096]{1,0:T(8,128)(2,1)S(1)} %collective-permute-done.1.refs_2_, bf16[16,4096]{1,0:T(8,128)(2,1)S(1)} %collective-permute-done.2.refs_3_, ...), custom_call_target="tpu_custom_call" | custom-call | flops 4294967296 | bytes 8388608 | tf_op jit(solution)/shard_map/attend/pallas_call | solution.py:200
  67.6 28.7 %all_to_all.14.refs_1_ = bf16[8,528,128]{2,1,0:T(8,128)(2,1)} all-to-all(bf16[8,528,128]{2,1,0:T(8,128)(2,1)S(1)} %attend.1), channel_id=1, replica_groups={{0,2,4,6,8,10,12,14},{1,3,5,7,9,11,13,15},{16,18,20,22,24,26,28,30},{17..., dimensions={0} | all-to-all | bytes 2162688 | tf_op jit(solution)/shard_map/all_to_all | solution.py:345
  96.4 8.9 %project.1 = (f32[8,8,8192]{2,1,0:T(8,128)}, bf16[64,8192]{1,0:T(8,128)(2,1)}) custom-call(s32[1]{0:T(128)} %bitcast.refs_0_, bf16[8,528,128]{2,1,0:T(8,128)(2,1)} %all_to_all.14.refs_1_, bf16[512,8192]{1,0:T(8,128)(2,1)} %refs_2_.1), custom_call_target="tpu_custom_call" | custom-call | flops 1073741824 | bytes 12582912 | tf_op jit(solution)/shard_map/project/pallas_call | solution.py:260
  105.3 2.9 %collective-permute-done.9 = bf16[64,8192]{1,0:T(8,128)(2,1)S(1)} collective-permute-done((bf16[64,8192]{1,0:T(8,128)(2,1)}, bf16[64,8192]{1,0:T(8,128)(2,1)S(1)}, u32[]{:S(2)}, u32[]{:S(2)}) %collective-permute-start.9) | collective-permute-done | bytes 1048608 | tf_op jit(solution)/shard_map/ppermute | solution.py:349
  108.2 1.8 %fusion.2 = bf16[8,8,8192]{2,1,0:T(8,128)(2,1)S(1)} fusion(bf16[64,8192]{1,0:T(8,128)(2,1)S(1)} %collective-permute-done.9, f32[8,8,8192]{2,1,0:T(8,128)} %get-tuple-element.7), kind=kLoop, calls=%fused_computation.7 | loop fusion | flops 1572864 | bytes 4194304 | tf_op jit(solution)/shard_map/all_to_all | solution.py:351
  110.0 28.7 %all_to_all.15 = bf16[8,8,8192]{2,1,0:T(8,128)(2,1)S(1)} all-to-all(bf16[8,8,8192]{2,1,0:T(8,128)(2,1)S(1)} %fusion.2), channel_id=1, replica_groups={{0,2,4,6,8,10,12,14},{1,3,5,7,9,11,13,15},{16,18,20,22,24,26,28,30},{17..., dimensions={0} | all-to-all | bytes 2097152 | tf_op jit(solution)/shard_map/all_to_all | solution.py:351
  138.7 0.8 reduce_sum.12
  (40 shorter events, 2.0 us)
Async XLA Ops:
  0.0 6.8 %copy-start = (bf16[16,8192]{1,0:T(8,128)(2,1)S(1)}, bf16[16,8192]{1,0:T(8,128)(2,1)}, u32[]{:S(2)}) copy-start(bf16[16,8192]{1,0:T(8,128)(2,1)} %param.11) | copy-start | bytes 786436
  0.0 7.2 %copy-start.8 = (s32[8]{0:T(128)S(1)}, s32[8]{0:T(128)}, u32[]{:S(2)}) copy-start(s32[8]{0:T(128)} %constant.60.clone) | copy-start | bytes 100
  0.0 6.8 %copy-start.6 = (s32[8]{0:T(128)S(1)}, s32[8]{0:T(128)}, u32[]{:S(2)}) copy-start(s32[8]{0:T(128)} %param.10) | copy-start | bytes 100
  0.0 6.8 %copy-start.4 = (bf16[8,8192]{1,0:T(8,128)(2,1)S(1)}, bf16[8,8192]{1,0:T(8,128)(2,1)}, u32[]{:S(2)}) copy-start(bf16[8,8192]{1,0:T(8,128)(2,1)} %param.9) | copy-start | bytes 393220
  6.3 26.3 %collective-permute-start.8 = (bf16[2,1024,1024]{1,2,0:T(8,128)(2,1)}, bf16[2,1024,1024]{1,2,0:T(8,128)(2,1)}, u32[]{:S(2)}, u32[]{:S(2)}) collective-permute-start(bf16[2,1024,1024]{1,2,0:T(8,128)(2,1)} %copy.22), channel_id=1, source_target_pairs={{0,1},{1,0},{2,3},{3,2},{4,5},{5,4},{6,7},{7,6},{8,9},{9,8},{10,11... | collective-permute-start | bytes 12582920 | tf_op jit(solution)/shard_map/ppermute | solution.py:313
  7.1 6.9 %collective-permute-start = (bf16[8,4096]{1,0:T(8,128)(2,1)S(1)}, bf16[8,4096]{1,0:T(8,128)(2,1)S(1)}, u32[]{:S(2)}, u32[]{:S(2)}) collective-permute-start(bf16[8,4096]{1,0:T(8,128)(2,1)S(1)} %bitcast.38), channel_id=1, source_target_pairs={{0,1},{1,0},{2,3},{3,2},{4,5},{5,4},{6,7},{7,6},{8,9},{9,8},{10,11... | collective-permute-start | bytes 196616 | tf_op jit(solution)/shard_map/ppermute | solution.py:309
  7.9 1.8 %copy-start.5 = (s32[2,128]{1,0:T(2,128)S(1)}, s32[2,128]{1,0:T(2,128)}, u32[]{:S(2)}) copy-start(s32[2,128]{1,0:T(2,128)} %param.13) | copy-start | bytes 3076
  7.9 14.6 %copy-start.7 = (s32[8]{0:T(128)S(1)}, s32[8]{0:T(128)}, u32[]{:S(2)}) copy-start(s32[8]{0:T(128)} %constant.61.clone) | copy-start | bytes 100
  7.9 19.9 %copy-start.3 = (s32[8]{0:T(128)S(1)}, s32[8]{0:T(128)}, u32[]{:S(2)}) copy-start(s32[8]{0:T(128)} %constant.59.clone) | copy-start | bytes 100
  14.0 6.7 %collective-permute-start.1 = (bf16[16,4096]{1,0:T(8,128)(2,1)S(1)}, bf16[16,4096]{1,0:T(8,128)(2,1)S(1)}, u32[]{:S(2)}, u32[]{:S(2)}) collective-permute-start(bf16[16,4096]{1,0:T(8,128)(2,1)S(1)} %pad_maximum_fusion.refs_1_), channel_id=1, source_target_pairs={{0,4},{1,5},{4,8},{5,9},{8,12},{9,13},{12,14},{13,15},{14,10},{15,... | collective-permute-start | bytes 393224 | tf_op jit(solution)/shard_map/ppermute | solution.py:323
  17.0 6.2 %collective-permute-start.2 = (bf16[16,4096]{1,0:T(8,128)(2,1)S(1)}, bf16[16,4096]{1,0:T(8,128)(2,1)S(1)}, u32[]{:S(2)}, u32[]{:S(2)}) collective-permute-start(bf16[16,4096]{1,0:T(8,128)(2,1)S(1)} %pad_maximum_fusion.refs_1_), channel_id=1, source_target_pairs={{0,2},{1,3},{4,0},{5,1},{8,4},{9,5},{12,8},{13,9},{14,12},{15,13},... | collective-permute-start | bytes 393224 | tf_op jit(solution)/shard_map/ppermute | solution.py:327
  20.7 5.0 %collective-permute-start.3 = (bf16[16,4096]{1,0:T(8,128)(2,1)S(1)}, bf16[16,4096]{1,0:T(8,128)(2,1)S(1)}, u32[]{:S(2)}, u32[]{:S(2)}) collective-permute-start(bf16[16,4096]{1,0:T(8,128)(2,1)S(1)} %collective-permute-done.1.refs_2_), channel_id=1, source_target_pairs={{0,4},{1,5},{4,8},{5,9},{8,12},{9,13},{12,14},{13,15},{14,10},{15,... | collective-permute-start | bytes 393224 | tf_op jit(solution)/shard_map/ppermute | solution.py:323
  23.2 5.3 %collective-permute-start.4 = (bf16[16,4096]{1,0:T(8,128)(2,1)S(1)}, bf16[16,4096]{1,0:T(8,128)(2,1)S(1)}, u32[]{:S(2)}, u32[]{:S(2)}) collective-permute-start(bf16[16,4096]{1,0:T(8,128)(2,1)S(1)} %collective-permute-done.2.refs_3_), channel_id=1, source_target_pairs={{0,2},{1,3},{4,0},{5,1},{8,4},{9,5},{12,8},{13,9},{14,12},{15,13},... | collective-permute-start | bytes 393224 | tf_op jit(solution)/shard_map/ppermute | solution.py:327
  25.7 5.0 %collective-permute-start.5 = (bf16[16,4096]{1,0:T(8,128)(2,1)S(1)}, bf16[16,4096]{1,0:T(8,128)(2,1)S(1)}, u32[]{:S(2)}, u32[]{:S(2)}) collective-permute-start(bf16[16,4096]{1,0:T(8,128)(2,1)S(1)} %collective-permute-done.3.refs_4_), channel_id=1, source_target_pairs={{0,4},{1,5},{4,8},{5,9},{8,12},{9,13},{12,14},{13,15},{14,10},{15,... | collective-permute-start | bytes 393224 | tf_op jit(solution)/shard_map/ppermute | solution.py:323
  28.4 13.5 %collective-permute-start.6 = (bf16[16,4096]{1,0:T(8,128)(2,1)S(1)}, bf16[16,4096]{1,0:T(8,128)(2,1)S(1)}, u32[]{:S(2)}, u32[]{:S(2)}) collective-permute-start(bf16[16,4096]{1,0:T(8,128)(2,1)S(1)} %collective-permute-done.4.refs_5_), channel_id=1, source_target_pairs={{0,2},{1,3},{4,0},{5,1},{8,4},{9,5},{12,8},{13,9},{14,12},{15,13},... | collective-permute-start | bytes 393224 | tf_op jit(solution)/shard_map/ppermute | solution.py:327
  30.6 11.3 %collective-permute-start.7 = (bf16[16,4096]{1,0:T(8,128)(2,1)S(1)}, bf16[16,4096]{1,0:T(8,128)(2,1)S(1)}, u32[]{:S(2)}, u32[]{:S(2)}) collective-permute-start(bf16[16,4096]{1,0:T(8,128)(2,1)S(1)} %collective-permute-done.5.refs_6_), channel_id=1, source_target_pairs={{0,4},{1,5},{4,8},{5,9},{8,12},{9,13},{12,14},{13,15},{14,10},{15,... | collective-permute-start | bytes 393224 | tf_op jit(solution)/shard_map/ppermute | solution.py:323
  42.0 2.2 %copy-start.1 = (bf16[2,1024,1024]{2,1,0:T(8,128)(2,1)S(1)}, bf16[2,1024,1024]{2,1,0:T(8,128)(2,1)}, u32[]{:S(2)}) copy-start(bf16[2,1024,1024]{2,1,0:T(8,128)(2,1)} %refs_9_.1) | copy-start | bytes 12582916
  44.2 1.6 %copy-start.2 = (bf16[1024,1024]{1,0:T(8,128)(2,1)S(1)}, bf16[1024,1024]{1,0:T(8,128)(2,1)}, u32[]{:S(2)}) copy-start(bf16[1024,1024]{1,0:T(8,128)(2,1)} %slice_bitcast_fusion.refs_12_) | copy-start | bytes 6291460
  105.3 2.9 %collective-permute-start.9 = (bf16[64,8192]{1,0:T(8,128)(2,1)}, bf16[64,8192]{1,0:T(8,128)(2,1)S(1)}, u32[]{:S(2)}, u32[]{:S(2)}) collective-permute-start(bf16[64,8192]{1,0:T(8,128)(2,1)} %get-tuple-element.8), channel_id=1, source_target_pairs={{0,1},{1,0},{2,3},{3,2},{4,5},{5,4},{6,7},{7,6},{8,9},{9,8},{10,11... | collective-permute-start | bytes 3145736 | tf_op jit(solution)/shard_map/ppermute | solution.py:349

commit v2 on v0

--- a/solution.py
+++ b/solution.py
@@ -1,6 +1,8 @@
 import jax
 import jax.numpy as jnp
 from jax import lax
+from jax.experimental import pallas as pl
+from jax.experimental.pallas import tpu as pltpu
 from jax.sharding import PartitionSpec as P
 
 HEADS = 64
@@ -109,9 +111,366 @@
     ).astype(jnp.bfloat16)
 
 
+NONE = -(2.0**100)
+LOG2E = 1.4426950408889634
+STAT_ROWS = 16
+ATTEND_VMEM = 60 * 1024 * 1024
+
+
+def pack_stats(peaks, totals):
+    high = [t.astype(jnp.bfloat16).astype(jnp.float32) for t in totals]
+    flat = peaks + high + [t - h for t, h in zip(totals, high)]
+    flat += [jnp.zeros_like(flat[0])] * (STAT_ROWS - len(flat))
+    return jnp.concatenate(flat, axis=0).astype(jnp.bfloat16)
+
+
+def unpack_stats(stats, heads):
+    stats = stats.astype(jnp.float32)
+    return stats[:heads], stats[heads : 2 * heads] + stats[2 * heads : 3 * heads]
+
+
+def attend_kernel(heads, tile, order, groups, *refs):
+    n_blocks, count = order.shape[0], groups.shape[0]
+    q_blocks = refs[: n_blocks * count]
+    sources = refs[n_blocks * count : n_blocks * count + 2]
+    keep = refs[n_blocks * count + 2]
+    outs = refs[n_blocks * count + 3 : n_blocks * count + 3 + count]
+    held, q_all, scores, acc, arrived = refs[n_blocks * count + 3 + count :]
+    block_rows = q_blocks[0].shape[0]
+    rows = n_blocks * block_rows
+    lanes = heads * rows
+    ctx = held.shape[1]
+    key_blocks, per_tile = ctx // BLOCK, tile // BLOCK
+    to_log2 = HEAD ** (-0.5) * LOG2E
+    units = [(i, s) for i in range(count) for s in range(2)]
+
+    def fetch(u, kind):
+        i, s = units[u]
+        column = pl.ds(pl.multiple_of(groups[i] * HEAD, HEAD), HEAD)
+        at = 2 * u + kind
+        return pltpu.make_async_copy(sources[s].at[kind, :, column], held.at[at], arrived.at[at])
+
+    for u in range(len(units)):
+        for kind in range(2):
+            fetch(u, kind).start()
+    for i in range(count):
+        for at in range(n_blocks):
+            for h in range(heads):
+                q_all[i, h, order[at]] = q_blocks[i * n_blocks + at][:, h * HEAD : (h + 1) * HEAD]
+
+    def score(u, t, peak):
+        i, s = units[u]
+        piece = lax.dot_general(
+            held[2 * u, t * tile : (t + 1) * tile, :],
+            q_all[i].reshape(lanes, HEAD),
+            (((1,), (1,)), ((), ())),
+            preferred_element_type=jnp.float32,
+        )
+        scores[u % 2, t * tile : (t + 1) * tile, :] = piece
+        for b in range(per_tile):
+            kept = keep[pl.ds(s * key_blocks + t * per_tile + b, 1), :]
+            part = piece[b * BLOCK : (b + 1) * BLOCK, :].reshape(BLOCK // 8, 8, lanes)
+            best = jnp.max(part, axis=0) * to_log2
+            peak = jnp.maximum(peak, jnp.where(kept > 0.0, best, NONE))
+        return peak
+
+    def weigh(u, t, peak, total):
+        s = units[u][1]
+        probs = []
+        for b in range(per_tile):
+            kept = keep[pl.ds(s * key_blocks + t * per_tile + b, 1), :]
+            shift = jnp.where(kept > 0.0, peak, -NONE)
+            low = t * tile + b * BLOCK
+            weights = jnp.exp2(scores[u % 2, low : low + BLOCK, :] * to_log2 - shift)
+            total = total + jnp.sum(weights.reshape(BLOCK // 8, 8, lanes), axis=0)
+            probs.append(weights.astype(jnp.bfloat16))
+        fresh = jnp.dot(
+            held[2 * u + 1, t * tile : (t + 1) * tile, :].T,
+            jnp.concatenate(probs, axis=0),
+            preferred_element_type=jnp.float32,
+        )
+        acc[s] = fresh if t == 0 else acc[s] + fresh
+        return total
+
+    tiles = range(ctx // tile)
+    lowest = jnp.full((8, lanes), NONE, jnp.float32)
+    fetch(0, 0).wait()
+    peak = lowest
+    for t in tiles:
+        peak = score(0, t, peak)
+    peaks, totals = [], []
+    for u, (i, s) in enumerate(units):
+        row = jnp.max(peak, axis=0, keepdims=True)
+        total = jnp.zeros((8, lanes), jnp.float32)
+        fetch(u, 1).wait()
+        peak = lowest
+        if u + 1 < len(units):
+            fetch(u + 1, 0).wait()
+        for t in tiles:
+            if u + 1 < len(units):
+                peak = score(u + 1, t, peak)
+            total = weigh(u, t, row, total)
+        peaks.append(row)
+        totals.append(jnp.sum(total, axis=0, keepdims=True))
+        if s == 1:
+            top = jnp.maximum(peaks[-2], peaks[-1]).astype(jnp.bfloat16).astype(jnp.float32)
+            scales = [jnp.exp2(p - top) for p in peaks[-2:]]
+            total = totals[-2] * scales[0] + totals[-1] * scales[1]
+            spans = [slice(h * rows, (h + 1) * rows) for h in range(heads)]
+            for h, span in enumerate(spans):
+                value = acc[0, :, span] * scales[0][:, span] + acc[1, :, span] * scales[1][:, span]
+                outs[i][h * HEAD : (h + 1) * HEAD, :] = value.astype(jnp.bfloat16)
+            outs[i][heads * HEAD :, :] = pack_stats(
+                [top[:, span] for span in spans], [total[:, span] for span in spans]
+            )
+
+
+def attend(q_blocks, order, groups, kv, kv_far, keep, heads, tile=256):
+    count = groups.shape[0]
+    n_blocks = len(q_blocks)
+    block_rows = q_blocks[0].shape[0]
+    rows = block_rows * n_blocks
+    ctx = kv.shape[1]
+    width = heads * HEAD
+    length = width + STAT_ROWS
+    return pl.pallas_call(
+        lambda *refs: attend_kernel(heads, tile, *refs),
+        grid_spec=pltpu.PrefetchScalarGridSpec(
+            num_scalar_prefetch=2,
+            grid=(1,),
+            in_specs=[
+                pl.BlockSpec((block_rows, width), lambda z, o, g, i=i: (0, g[i]))
+                for i in range(count)
+                for _ in q_blocks
+            ]
+            + [pl.BlockSpec(memory_space=pl.ANY)] * 2
+            + [pl.BlockSpec(keep.shape, lambda z, o, g: (0, 0))],
+            out_specs=[pl.BlockSpec((length, rows), lambda z, o, g: (0, 0)) for _ in range(count)],
+            scratch_shapes=[
+                pltpu.VMEM((4 * count, ctx, HEAD), jnp.bfloat16),
+                pltpu.VMEM((count, heads, n_blocks, block_rows, HEAD), jnp.bfloat16),
+                pltpu.VMEM((2, ctx, heads * rows), jnp.float32),
+                pltpu.VMEM((2, HEAD, heads * rows), jnp.float32),
+                pltpu.SemaphoreType.DMA((4 * count,)),
+            ],
+        ),
+        out_shape=[jax.ShapeDtypeStruct((length, rows), jnp.bfloat16) for _ in range(count)],
+        compiler_params=pltpu.CompilerParams(
+            dimension_semantics=("arbitrary",), vmem_limit_bytes=ATTEND_VMEM
+        ),
+        cost_estimate=pl.CostEstimate(
+            flops=12 * count * rows * width * 2 * ctx,
+            bytes_accessed=8 * count * ctx * HEAD,
+            transcendentals=count * rows * heads * 2 * ctx,
+        ),
+        name="attend",
+    )(order, groups, *(list(q_blocks) * count), kv, kv_far, keep)
+
+
+def merge_parts(parts, heads):
+    stats = [unpack_stats(p[heads * HEAD :, :], heads) for p in parts]
+    top = stats[0][0]
+    for peaks, _ in stats[1:]:
+        top = jnp.maximum(top, peaks)
+    scales = [jnp.exp2(peaks - top) for peaks, _ in stats]
+    total = sum(w * t for w, (_, t) in zip(scales, stats))
+    values = []
+    for h in range(heads):
+        place = slice(h * HEAD, (h + 1) * HEAD)
+        values.append(
+            sum(w[h : h + 1] * p[place, :].astype(jnp.float32) for w, p in zip(scales, parts))
+        )
+    return top, total, values
+
+
+def merge_kernel(heads, pairs, *refs):
+    for p in range(pairs):
+        near, came, out = refs[2 * p], refs[2 * p + 1], refs[2 * pairs + p]
+        top, total, values = merge_parts([near, came], heads)
+        for h in range(heads):
+            out[h * HEAD : (h + 1) * HEAD, :] = values[h].astype(jnp.bfloat16)
+        rows = [slice(h, h + 1) for h in range(heads)]
+        out[heads * HEAD :, :] = pack_stats([top[r] for r in rows], [total[r] for r in rows])
+
+
+def merge(pairs, heads):
+    shape = pairs[0][0].shape
+    spec = pl.BlockSpec(shape, lambda: (0, 0))
+    return pl.pallas_call(
+        lambda *refs: merge_kernel(heads, len(pairs), *refs),
+        in_specs=[spec] * (2 * len(pairs)),
+        out_specs=[spec] * len(pairs),
+        out_shape=[jax.ShapeDtypeStruct(shape, jnp.bfloat16)] * len(pairs),
+        compiler_params=pltpu.CompilerParams(vmem_limit_bytes=ATTEND_VMEM),
+        cost_estimate=pl.CostEstimate(
+            flops=1000000, bytes_accessed=6 * shape[0] * shape[1] * len(pairs), transcendentals=0
+        ),
+        name="merge",
+    )(*[x for pair in pairs for x in pair])
+
+
+def project_kernel(heads, core, *refs):
+    parts, (w_ref, kept, sent, attended) = refs[:-4], refs[-4:]
+
+    @pl.when(pl.program_id(0) == 0)
+    def _():
+        _, total, values = merge_parts(parts, heads)
+        for h in range(heads):
+            mean = values[h] / total[h : h + 1]
+            attended[:, h * HEAD : (h + 1) * HEAD] = mean.T.astype(jnp.bfloat16)
+
+    full = jnp.dot(attended[...], w_ref[...], preferred_element_type=jnp.float32)
+    chips, per_dev, tile = kept.shape
+    full = full.reshape(chips, 2, per_dev, tile)
+    first = core[0] == 0
+    kept[...] = jnp.where(first, full[:, 0], full[:, 1])
+    away = jnp.where(first, full[:, 1], full[:, 0])
+    sent[...] = away.reshape(chips * per_dev, tile).astype(jnp.bfloat16)
+
+
+def project(parts, core, w_out, heads, per_dev, part, part_count, tile=1024):
+    length, rows = parts[0].shape
+    chips = rows // (2 * per_dev)
+    cols = w_out.shape[1] // part_count
+    steps = cols // tile
+    return pl.pallas_call(
+        lambda *refs: project_kernel(heads, *refs),
+        grid_spec=pltpu.PrefetchScalarGridSpec(
+            num_scalar_prefetch=1,
+            grid=(steps,),
+            in_specs=[pl.BlockSpec((length, rows), lambda j, c: (0, 0)) for _ in parts]
+            + [pl.BlockSpec((heads * HEAD, tile), lambda j, c: (0, j + part * steps))],
+            out_specs=[
+                pl.BlockSpec((chips, per_dev, tile), lambda j, c: (0, 0, j)),
+                pl.BlockSpec((chips * per_dev, tile), lambda j, c: (0, j)),
+            ],
+            scratch_shapes=[pltpu.VMEM((rows, heads * HEAD), jnp.bfloat16)],
+        ),
+        out_shape=[
+            jax.ShapeDtypeStruct((chips, per_dev, cols), jnp.float32),
+            jax.ShapeDtypeStruct((chips * per_dev, cols), jnp.bfloat16),
+        ],
+        compiler_params=pltpu.CompilerParams(dimension_semantics=("arbitrary",)),
+        cost_estimate=pl.CostEstimate(
+            flops=2 * rows * heads * HEAD * cols,
+            bytes_accessed=3 * heads * HEAD * cols,
+            transcendentals=0,
+        ),
+        name="project",
+    )(core, *parts, w_out)
+
+
+def paired_device(queries, steer_ids, steer_table, kv, blocks, w_out):
+    n = lax.axis_size("ctx")
+    me = lax.axis_index("ctx")
+    chips = n // 2
+    core = me % 2
+    chip = me // 2
+    per_dev = queries.shape[0]
+    rows = per_dev * n
+    width = D // n
+    heads = width // HEAD
+    swap = [(i, i ^ 1) for i in range(n)]
+    ring = list(range(0, chips, 2)) + list(range(chips - 1, 0, -2))
+
+    def hop(step):
+        return [
+            (2 * ring[p] + c, 2 * ring[(p + step) % chips] + c) for p in range(chips) for c in range(2)
+        ]
+
+    ahead_pairs, behind_pairs = hop(1), hop(-1)
+    place = jnp.where(chip % 2 == 0, chip // 2, chips - 1 - chip // 2)
+
+    def chip_at(offset):
+        p = (place + offset) % chips
+        return jnp.where(p < chips // 2, 2 * p, 2 * (chips - 1 - p) + 1)
+
+    steered = apply_steer(queries, steer_ids, steer_table)
+    halves = steered.reshape(per_dev, chips, 2, width)
+    mine = jnp.where(core == 0, halves[:, :, 0], halves[:, :, 1]).reshape(per_dev, D // 2)
+    other = jnp.where(core == 0, halves[:, :, 1], halves[:, :, 0]).reshape(per_dev, D // 2)
+    theirs = lax.ppermute(other, "ctx", swap)
+    block = jnp.concatenate(
+        [jnp.where(core == 0, mine, theirs), jnp.where(core == 0, theirs, mine)], axis=0
+    )
+    found, offsets = [block], [0]
+    ahead, behind = block, block
+    for s in range(1, chips // 2 + 1):
+        ahead = lax.ppermute(ahead, "ctx", ahead_pairs)
+        found.append(ahead)
+        offsets.append(-s)
+        if s < chips - s:
+            behind = lax.ppermute(behind, "ctx", behind_pairs)
+            found.append(behind)
+            offsets.append(s)
+        if s == 1:
+            ahead, kv_late, blocks_late = lax.optimization_barrier((ahead, kv, blocks))
+            kv_far = lax.ppermute(kv_late, "ctx", swap)
+    order = chip_at(jnp.array(offsets, jnp.int32))
+
+    block_count = kv.shape[1] // BLOCK
+    ids = jnp.arange(2 * block_count, dtype=jnp.int32)
+    ids = jnp.where(ids < block_count, me * block_count + ids, (me ^ 1) * block_count + ids - block_count)
+    hits = jnp.any(blocks_late[:, None, :] == ids[None, :, None], axis=2)
+    keep = jnp.repeat(hits.T.astype(jnp.float32), BLOCK, axis=1)
+    keep = jnp.concatenate([keep] * heads, axis=1)
+
+    half = chips // 2
+
+    def attend_for(targets):
+        groups = chip_at(jnp.array(targets, jnp.int32))
+        return attend(found, order, groups, kv, kv_far, keep, heads)
+
+    went_ahead, went_behind = None, None
+    for s in range(1, half + 1):
+        outs = attend_for([half + 1 - s] + ([s - 1 - half] if s > 1 else []))
+        came = [went_ahead, went_behind]
+        pairs = [(x, y) for x, y in zip(outs, came) if y is not None]
+        if pairs:
+            merged = merge(pairs, heads)
+            outs = list(merged) + list(outs[len(merged) :])
+        went_ahead = lax.ppermute(outs[0], "ctx", ahead_pairs)
+        if s > 1:
+            went_behind = lax.ppermute(outs[1], "ctx", behind_pairs)
+    parts = [attend_for([0])[0], went_ahead, went_behind]
+
+    col_parts = 2
+    pieces = []
+    for h in range(col_parts):
+        kept, sent = project(parts, core.reshape(1), w_out, heads, per_dev, h, col_parts)
+        got = lax.ppermute(sent, "ctx", swap).reshape(kept.shape)
+        pieces.append((kept, got))
+
+    def term(piece, offset):
+        at = chip_at(offset)
+        pick = [lax.dynamic_index_in_dim(x, at, 0, keepdims=False) for x in piece]
+        return pick[0] + pick[1].astype(jnp.float32)
+
+    streams = [[None, None] for _ in pieces]
+    for s in range(1, half + 1):
+        for h, piece in enumerate(pieces):
+            came_ahead, came_behind = streams[h]
+            total = term(piece, half + 1 - s)
+            if came_ahead is not None:
+                total = total + came_ahead.astype(jnp.float32)
+            streams[h][0] = lax.ppermute(total.astype(jnp.bfloat16), "ctx", ahead_pairs)
+            if s > 1:
+                total = term(piece, s - 1 - half)
+                if came_behind is not None:
+                    total = total + came_behind.astype(jnp.float32)
+                streams[h][1] = lax.ppermute(total.astype(jnp.bfloat16), "ctx", behind_pairs)
+    done = []
+    for piece, (came_ahead, came_behind) in zip(pieces, streams):
+        total = term(piece, 0) + came_ahead.astype(jnp.float32) + came_behind.astype(jnp.float32)
+        done.append(total.astype(jnp.bfloat16))
+    return jnp.concatenate(done, axis=1)
+
+
 def solution(mesh):
+    n = mesh.shape["ctx"]
+    paired = n == 2 * KV_HEADS
     return jax.shard_map(
-        per_device,
+        paired_device if paired else per_device,
         mesh=mesh,
         in_specs=(
             P(("parts", "ctx"), None),

time: 326 us -> 118 us (0.36)
  waiting for transfers between devices: 205 us -> 19.4 us
  matrix products: 50.6 us -> 1.15 us
  Pallas kernels: 0 us -> 44.2 us
  starting transfers between devices: 11.8 us -> 35.8 us
  local copies, waits for them, and re-layouts: 28 us -> 4.6 us
  between operations: 13.5 us -> 0.34 us
  other arithmetic: 14.8 us -> 11.2 us
    reduce_scatter x1 -> x0, waiting for transfers between devices: 87.8 us -> none  [per_device(): lax.psum_scatter(jnp.dot(attended, w_out, preferred_element_type=jnp.floa...]
    all_to_all x3 -> x0, waiting for transfers between devices: 84.6 us -> none  [the longest x1 77.4 us: per_device(): lax.all_to_all(outs, 'ctx', split_axis=1, concat_axis=0, tiled=True)]
    dot_general x17 -> x0, matrix products: 48.8 us -> none  [the longest x8 25.8 us: group_attend(): partial_out = jnp.dot(probs, v_rows, preferred_element_type=jnp.float32)]
    pallas_call x0 -> x10, Pallas kernels: none -> 44.2 us  [the longest x5 28.6 us: attend(): pl.pallas_call(lambda *refs: attend_kernel(heads, tile, *refs), grid_spec...]
    ppermute x0 -> x32, starting transfers between devices: none -> 35.8 us  [the longest x8 12.4 us: paired_device(): streams[h][0] = lax.ppermute(total.astype(jnp.bfloat16), 'ctx', ahead_pairs)]
    all_gather x1 -> x0, waiting for transfers between devices: 32.8 us -> none  [per_device(): steered = lax.all_gather(steered_local, 'ctx', axis=0, tiled=True)]
    ppermute x0 -> x32, waiting for transfers between devices: none -> 19.4 us  [the longest x3 8.68 us: paired_device(): behind = lax.ppermute(behind, 'ctx', behind_pairs)]
    reduce_sum x10 -> x0, other arithmetic: 13 us -> none  [the longest x8 10.4 us: group_attend(): row_total = jnp.sum(weights, axis=1)]
  transfers between devices with their start and end apart: 5 -> 32, of which waited for: 5 -> 11; matrix products, arithmetic and copies ran while one was open for 5% -> 8% of each run, Pallas kernels for 0% -> 26%
where the time goes in v2:
time: 118 us; the launch traced here: 117 us
  Pallas kernels  44.2 us (37%)
  starting transfers between devices  35.8 us (30%)
  waiting for transfers between devices  19.4 us (16%)
  other arithmetic  11.2 us (9%)
  local copies, waits for them, and re-layouts  4.6 us (4%)
    pallas_call x5, Pallas kernels, attend(): pl.pallas_call(lambda *refs: attend_kernel(heads, tile, *refs), grid_spec...  28.6 us
    ppermute x8, starting transfers between devices, paired_device(): streams[h][0] = lax.ppermute(total.astype(jnp.bfloat16), 'ctx', ahead_pairs)  12.4 us
    pallas_call x2, Pallas kernels, project(): pl.pallas_call(lambda *refs: project_kernel(heads, *refs), grid_spec=pltp...  10 us
    ppermute x3, waiting for transfers between devices, paired_device(): behind = lax.ppermute(behind, 'ctx', behind_pairs)  8.68 us
    ppermute x6, starting transfers between devices, paired_device(): lax.ppermute(total.astype(jnp.bfloat16), 'ctx', behind_pairs)  6.8 us
    pallas_call x3, Pallas kernels, merge(): pl.pallas_call(lambda *refs: merge_kernel(heads, len(pairs), *refs), in_s...  5.52 us
    ppermute x4, waiting for transfers between devices, paired_device(): ahead = lax.ppermute(ahead, 'ctx', ahead_pairs)  5.4 us
    ppermute x3, starting transfers between devices, paired_device(): behind = lax.ppermute(behind, 'ctx', behind_pairs)  5.06 us
  transfers between devices with their start and end apart: 32, of which 11 were waited for; matrix products, arithmetic and copies ran while one was open for 8% of the time, Pallas kernels for 26%

profile of v2, /device:TPU:0, one launch (start us, length us, event | category | flops | bytes accessed | tf_op | source)
XLA Modules:
  0.0 116.7 jit_solution(11494591723110864976)
XLA Ops:
  3.6 3.0 %collective-permute-start.1 = (bf16[16,4096]{1,0:T(8,128)(2,1)S(1)}, bf16[16,4096]{1,0:T(8,128)(2,1)S(1)}, u32[]{:S(2)}, u32[]{:S(2)}) collective-permute-start(bf16[16,4096]{1,0:T(8,128)(2,1)S(1)} %pad_maximum_fusion.refs_2_.refs_10_), channel_id=1, source_target_pairs={{0,4},{1,5},{4,8},{5,9},{8,12},{9,13},{12,14},{13,15},{14,10},{15,... | collective-permute-start | bytes 393224 | tf_op jit(solution)/shard_map/ppermute | solution.py:399
  6.6 3.8 %collective-permute-done.1.refs_3_.refs_11_ = bf16[16,4096]{1,0:T(8,128)(2,1)S(1)} collective-permute-done((bf16[16,4096]{1,0:T(8,128)(2,1)S(1)}, bf16[16,4096]{1,0:T(8,128)(2,1)S(1)}, u32[]{:S(2)}, u32[]{:S(2)}) %collective-permute-start.1) | collective-permute-done | bytes 131104 | tf_op jit(solution)/shard_map/ppermute | solution.py:399
  14.1 1.7 %collective-permute-start.2 = (bf16[16,4096]{1,0:T(8,128)(2,1)S(1)}, bf16[16,4096]{1,0:T(8,128)(2,1)S(1)}, u32[]{:S(2)}, u32[]{:S(2)}) collective-permute-start(bf16[16,4096]{1,0:T(8,128)(2,1)S(1)} %pad_maximum_fusion.refs_2_.refs_10_), channel_id=1, source_target_pairs={{0,2},{1,3},{4,0},{5,1},{8,4},{9,5},{12,8},{13,9},{14,12},{15,13},... | collective-permute-start | bytes 393224 | tf_op jit(solution)/shard_map/ppermute | solution.py:403
  17.3 2.7 %collective-permute-done.2.refs_4_.refs_12_ = bf16[16,4096]{1,0:T(8,128)(2,1)S(1)} collective-permute-done((bf16[16,4096]{1,0:T(8,128)(2,1)S(1)}, bf16[16,4096]{1,0:T(8,128)(2,1)S(1)}, u32[]{:S(2)}, u32[]{:S(2)}) %collective-permute-start.2) | collective-permute-done | bytes 131104 | tf_op jit(solution)/shard_map/ppermute | solution.py:403
  22.1 3.0 %collective-permute-done.4.refs_6_.refs_14_ = bf16[16,4096]{1,0:T(8,128)(2,1)S(1)} collective-permute-done((bf16[16,4096]{1,0:T(8,128)(2,1)S(1)}, bf16[16,4096]{1,0:T(8,128)(2,1)S(1)}, u32[]{:S(2)}, u32[]{:S(2)}) %collective-permute-start.4) | collective-permute-done | bytes 131104 | tf_op jit(solution)/shard_map/ppermute | solution.py:403
  27.1 2.9 %collective-permute-done.6.refs_8_.refs_16_ = bf16[16,4096]{1,0:T(8,128)(2,1)S(1)} collective-permute-done((bf16[16,4096]{1,0:T(8,128)(2,1)S(1)}, bf16[16,4096]{1,0:T(8,128)(2,1)S(1)}, u32[]{:S(2)}, u32[]{:S(2)}) %collective-permute-start.6) | collective-permute-done | bytes 131104 | tf_op jit(solution)/shard_map/ppermute | solution.py:403
  32.3 4.9 %attend.9 = bf16[528,128]{1,0:T(8,128)(2,1)} custom-call(s32[8]{0:T(128)} %compare_select_fusion.12.refs_0_, s32[1]{0:T(128)S(6)} %select_n.268.refs_1_, bf16[16,4096]{1,0:T(8,128)(2,1)} %copy-done.1, bf16[16,4096]{1,0:T(8,128)(2,1)} %copy-done.5, bf16[16,4096]{1,0:T(8,128)(2,1)} %copy-done.6, bf16[16,4096]{1,0:T(8,128)(2,1)} %copy-done.7, ...), custom_call_target="tpu_custom_call" | custom-call | flops 1610612736 | bytes 1048576 | tf_op jit(solution)/shard_map/attend/pallas_call | solution.py:236
  37.7 6.3 %attend.8 = (bf16[528,128]{1,0:T(8,128)(2,1)}, bf16[528,128]{1,0:T(8,128)(2,1)}) custom-call(s32[8]{0:T(128)} %compare_select_fusion.12.refs_0_, s32[2]{0:T(128)} %get-tuple-element.51.refs_1_, bf16[16,4096]{1,0:T(8,128)(2,1)} %copy-done.1, bf16[16,4096]{1,0:T(8,128)(2,1)} %copy-done.5, bf16[16,4096]{1,0:T(8,128)(2,1)} %copy-done.6, ...), custom_call_target="tpu_custom_call" | custom-call | flops 3221225472 | bytes 2097152 | tf_op jit(solution)/shard_map/attend/pallas_call | solution.py:236
  46.4 1.7 %merge.3 = bf16[528,128]{1,0:T(8,128)(2,1)} custom-call(bf16[528,128]{1,0:T(8,128)(2,1)} %get-tuple-element.27.refs_0_, bf16[528,128]{1,0:T(8,128)(2,1)} %copy-done.13), custom_call_target="tpu_custom_call" | custom-call | flops 1000000 | bytes 405504 | tf_op jit(solution)/shard_map/merge/pallas_call | solution.py:299
  48.4 6.3 %attend.7 = (bf16[528,128]{1,0:T(8,128)(2,1)}, bf16[528,128]{1,0:T(8,128)(2,1)}) custom-call(s32[8]{0:T(128)} %compare_select_fusion.12.refs_0_, s32[2]{0:T(128)} %get-tuple-element.52.refs_1_, bf16[16,4096]{1,0:T(8,128)(2,1)} %copy-done.1, bf16[16,4096]{1,0:T(8,128)(2,1)} %copy-done.5, bf16[16,4096]{1,0:T(8,128)(2,1)} %copy-done.6, ...), custom_call_target="tpu_custom_call" | custom-call | flops 3221225472 | bytes 2097152 | tf_op jit(solution)/shard_map/attend/pallas_call | solution.py:236
  55.4 1.9 %merge.4 = (bf16[528,128]{1,0:T(8,128)(2,1)}, bf16[528,128]{1,0:T(8,128)(2,1)}) custom-call(bf16[528,128]{1,0:T(8,128)(2,1)} %get-tuple-element.26.refs_0_, bf16[528,128]{1,0:T(8,128)(2,1)} %copy-done.16, bf16[528,128]{1,0:T(8,128)(2,1)} %get-tuple-element.28.refs_2_, bf16[528,128]{1,0:T(8,128)(2,1)} %copy-done.14), custom_call_target="tpu_custom_call" | custom-call | flops 1000000 | bytes 811008 | tf_op jit(solution)/shard_map/merge/pallas_call | solution.py:299
  59.4 6.3 %attend.6 = (bf16[528,128]{1,0:T(8,128)(2,1)}, bf16[528,128]{1,0:T(8,128)(2,1)}) custom-call(s32[8]{0:T(128)} %compare_select_fusion.12.refs_0_, s32[2]{0:T(128)} %compare_select_fusion.10.refs_1_, bf16[16,4096]{1,0:T(8,128)(2,1)} %copy-done.1, bf16[16,4096]{1,0:T(8,128)(2,1)} %copy-done.5, bf16[16,4096]{1,0:T(8,128)(2,1)} %copy-done.6, ...), custom_call_target="tpu_custom_call" | custom-call | flops 3221225472 | bytes 2097152 | tf_op jit(solution)/shard_map/attend/pallas_call | solution.py:236
  66.4 1.9 %merge.5 = (bf16[528,128]{1,0:T(8,128)(2,1)}, bf16[528,128]{1,0:T(8,128)(2,1)}) custom-call(bf16[528,128]{1,0:T(8,128)(2,1)} %get-tuple-element.25.refs_0_, bf16[528,128]{1,0:T(8,128)(2,1)} %copy-done.15, bf16[528,128]{1,0:T(8,128)(2,1)} %get-tuple-element.31.refs_2_, bf16[528,128]{1,0:T(8,128)(2,1)} %copy-done.17), custom_call_target="tpu_custom_call" | custom-call | flops 1000000 | bytes 811008 | tf_op jit(solution)/shard_map/merge/pallas_call | solution.py:299
  70.4 4.9 %attend.5.refs_1_ = bf16[528,128]{1,0:T(8,128)(2,1)} custom-call(s32[8]{0:T(128)} %compare_select_fusion.12.refs_0_, s32[1]{0:T(128)S(6)} %select_n.251.refs_1_, bf16[16,4096]{1,0:T(8,128)(2,1)} %copy-done.1, bf16[16,4096]{1,0:T(8,128)(2,1)} %copy-done.5, bf16[16,4096]{1,0:T(8,128)(2,1)} %copy-done.6, bf16[16,4096]{1,0:T(8,128)(2,1)} %copy-done.7, ...), custom_call_target="tpu_custom_call" | custom-call | flops 1610612736 | bytes 1048576 | tf_op jit(solution)/shard_map/attend/pallas_call | solution.py:236
  76.0 5.0 %project.2 = (f32[8,8,4096]{2,1,0:T(8,128)}, bf16[64,4096]{1,0:T(8,128)(2,1)}) custom-call(s32[1]{0:T(128)} %bitcast.refs_0_, bf16[528,128]{1,0:T(8,128)(2,1)} %attend.5.refs_1_, bf16[528,128]{1,0:T(8,128)(2,1)} %copy-done.3, bf16[528,128]{1,0:T(8,128)(2,1)} %copy-done.4, bf16[512,8192]{1,0:T(8,128)(2,1)} %refs_4_.3), custom_call_target="tpu_custom_call" | custom-call | flops 536870912 | bytes 6291456 | tf_op jit(solution)/shard_map/project/pallas_call | solution.py:336
  81.0 5.1 %project.3 = (f32[8,8,4096]{2,1,0:T(8,128)}, bf16[64,4096]{1,0:T(8,128)(2,1)}) custom-call(s32[1]{0:T(128)} %bitcast.refs_0_, bf16[528,128]{1,0:T(8,128)(2,1)} %attend.5.refs_1_, bf16[528,128]{1,0:T(8,128)(2,1)} %copy-done.3, bf16[528,128]{1,0:T(8,128)(2,1)} %copy-done.4, bf16[512,8192]{1,0:T(8,128)(2,1)} %refs_4_.3), custom_call_target="tpu_custom_call" | custom-call | flops 536870912 | bytes 6291456 | tf_op jit(solution)/shard_map/project/pallas_call | solution.py:336
  86.5 1.7 %collective-permute-start.17 = (bf16[8,4096]{1,0:T(8,128)(2,1)S(1)}, bf16[8,4096]{1,0:T(8,128)(2,1)S(1)}, u32[]{:S(2)}, u32[]{:S(2)}) collective-permute-start(bf16[8,4096]{1,0:T(8,128)(2,1)S(1)} %get-tuple-element.41), channel_id=1, source_target_pairs={{0,4},{1,5},{4,8},{5,9},{8,12},{9,13},{12,14},{13,15},{14,10},{15,... | collective-permute-start | bytes 196616 | tf_op jit(solution)/shard_map/ppermute | solution.py:456
  89.6 1.7 %collective-permute-start.25 = (bf16[8,4096]{1,0:T(8,128)(2,1)S(1)}, bf16[8,4096]{1,0:T(8,128)(2,1)S(1)}, u32[]{:S(2)}, u32[]{:S(2)}) collective-permute-start(bf16[8,4096]{1,0:T(8,128)(2,1)S(1)} %get-tuple-element.45), channel_id=1, source_target_pairs={{0,4},{1,5},{4,8},{5,9},{8,12},{9,13},{12,14},{13,15},{14,10},{15,... | collective-permute-start | bytes 196616 | tf_op jit(solution)/shard_map/ppermute | solution.py:456
  91.7 1.7 %collective-permute-start.18 = (bf16[8,4096]{1,0:T(8,128)(2,1)S(1)}, bf16[8,4096]{1,0:T(8,128)(2,1)S(1)}, u32[]{:S(2)}, u32[]{:S(2)}) collective-permute-start(bf16[8,4096]{1,0:T(8,128)(2,1)S(1)} %fusion.10), channel_id=1, source_target_pairs={{0,4},{1,5},{4,8},{5,9},{8,12},{9,13},{12,14},{13,15},{14,10},{15,... | collective-permute-start | bytes 196616 | tf_op jit(solution)/shard_map/ppermute | solution.py:456
  94.9 1.7 %collective-permute-start.26 = (bf16[8,4096]{1,0:T(8,128)(2,1)S(1)}, bf16[8,4096]{1,0:T(8,128)(2,1)S(1)}, u32[]{:S(2)}, u32[]{:S(2)}) collective-permute-start(bf16[8,4096]{1,0:T(8,128)(2,1)S(1)} %fusion.3), channel_id=1, source_target_pairs={{0,4},{1,5},{4,8},{5,9},{8,12},{9,13},{12,14},{13,15},{14,10},{15,... | collective-permute-start | bytes 196616 | tf_op jit(solution)/shard_map/ppermute | solution.py:456
  100.2 1.7 %collective-permute-start.27 = (bf16[8,4096]{1,0:T(8,128)(2,1)S(1)}, bf16[8,4096]{1,0:T(8,128)(2,1)S(1)}, u32[]{:S(2)}, u32[]{:S(2)}) collective-permute-start(bf16[8,4096]{1,0:T(8,128)(2,1)S(1)} %fusion.4), channel_id=1, source_target_pairs={{0,4},{1,5},{4,8},{5,9},{8,12},{9,13},{12,14},{13,15},{14,10},{15,... | collective-permute-start | bytes 196616 | tf_op jit(solution)/shard_map/ppermute | solution.py:456
  105.5 1.7 %collective-permute-start.30 = (bf16[8,4096]{1,0:T(8,128)(2,1)S(1)}, bf16[8,4096]{1,0:T(8,128)(2,1)S(1)}, u32[]{:S(2)}, u32[]{:S(2)}) collective-permute-start(bf16[8,4096]{1,0:T(8,128)(2,1)S(1)} %get-tuple-element.44), channel_id=1, source_target_pairs={{0,2},{1,3},{4,0},{5,1},{8,4},{9,5},{12,8},{13,9},{14,12},{15,13},... | collective-permute-start | bytes 196616 | tf_op jit(solution)/shard_map/ppermute | solution.py:461
  110.8 2.4 %collective-permute-start.31 = (bf16[8,4096]{1,0:T(8,128)(2,1)S(1)}, bf16[8,4096]{1,0:T(8,128)(2,1)S(1)}, u32[]{:S(2)}, u32[]{:S(2)}) collective-permute-start(bf16[8,4096]{1,0:T(8,128)(2,1)S(1)} %fusion.2), channel_id=1, source_target_pairs={{0,2},{1,3},{4,0},{5,1},{8,4},{9,5},{12,8},{13,9},{14,12},{15,13},... | collective-permute-start | bytes 196616 | tf_op jit(solution)/shard_map/ppermute | solution.py:461
  113.2 1.9 %collective-permute-done.31 = bf16[8,4096]{1,0:T(8,128)(2,1)S(1)} collective-permute-done((bf16[8,4096]{1,0:T(8,128)(2,1)S(1)}, bf16[8,4096]{1,0:T(8,128)(2,1)S(1)}, u32[]{:S(2)}, u32[]{:S(2)}) %collective-permute-start.31) | collective-permute-done | bytes 65568 | tf_op jit(solution)/shard_map/ppermute | solution.py:461
  (116 shorter events, 40.4 us)
Async XLA Ops:
  3.6 6.7 %collective-permute-start.1 = (bf16[16,4096]{1,0:T(8,128)(2,1)S(1)}, bf16[16,4096]{1,0:T(8,128)(2,1)S(1)}, u32[]{:S(2)}, u32[]{:S(2)}) collective-permute-start(bf16[16,4096]{1,0:T(8,128)(2,1)S(1)} %pad_maximum_fusion.refs_2_.refs_10_), channel_id=1, source_target_pairs={{0,4},{1,5},{4,8},{5,9},{8,12},{9,13},{12,14},{13,15},{14,10},{15,... | collective-permute-start | bytes 393224 | tf_op jit(solution)/shard_map/ppermute | solution.py:399
  10.4 21.3 %collective-permute-start.8 = (bf16[2,1024,1024]{2,1,0:T(8,128)(2,1)}, bf16[2,1024,1024]{2,1,0:T(8,128)(2,1)}, u32[]{:S(2)}, u32[]{:S(2)}) collective-permute-start(bf16[2,1024,1024]{2,1,0:T(8,128)(2,1)} %refs_10_.3), channel_id=1, source_target_pairs={{0,1},{1,0},{2,3},{3,2},{4,5},{5,4},{6,7},{7,6},{8,9},{9,8},{10,11... | collective-permute-start | bytes 12582920 | tf_op jit(solution)/shard_map/ppermute | solution.py:408
  14.1 5.9 %collective-permute-start.2 = (bf16[16,4096]{1,0:T(8,128)(2,1)S(1)}, bf16[16,4096]{1,0:T(8,128)(2,1)S(1)}, u32[]{:S(2)}, u32[]{:S(2)}) collective-permute-start(bf16[16,4096]{1,0:T(8,128)(2,1)S(1)} %pad_maximum_fusion.refs_2_.refs_10_), channel_id=1, source_target_pairs={{0,2},{1,3},{4,0},{5,1},{8,4},{9,5},{12,8},{13,9},{14,12},{15,13},... | collective-permute-start | bytes 393224 | tf_op jit(solution)/shard_map/ppermute | solution.py:403
  15.9 5.9 %collective-permute-start.3 = (bf16[16,4096]{1,0:T(8,128)(2,1)S(1)}, bf16[16,4096]{1,0:T(8,128)(2,1)S(1)}, u32[]{:S(2)}, u32[]{:S(2)}) collective-permute-start(bf16[16,4096]{1,0:T(8,128)(2,1)S(1)} %collective-permute-done.1.refs_3_.refs_11_), channel_id=1, source_target_pairs={{0,4},{1,5},{4,8},{5,9},{8,12},{9,13},{12,14},{13,15},{14,10},{15,... | collective-permute-start | bytes 393224 | tf_op jit(solution)/shard_map/ppermute | solution.py:399
  20.0 5.1 %collective-permute-start.4 = (bf16[16,4096]{1,0:T(8,128)(2,1)S(1)}, bf16[16,4096]{1,0:T(8,128)(2,1)S(1)}, u32[]{:S(2)}, u32[]{:S(2)}) collective-permute-start(bf16[16,4096]{1,0:T(8,128)(2,1)S(1)} %collective-permute-done.2.refs_4_.refs_12_), channel_id=1, source_target_pairs={{0,2},{1,3},{4,0},{5,1},{8,4},{9,5},{12,8},{13,9},{14,12},{15,13},... | collective-permute-start | bytes 393224 | tf_op jit(solution)/shard_map/ppermute | solution.py:403
  21.7 5.0 %collective-permute-start.5 = (bf16[16,4096]{1,0:T(8,128)(2,1)S(1)}, bf16[16,4096]{1,0:T(8,128)(2,1)S(1)}, u32[]{:S(2)}, u32[]{:S(2)}) collective-permute-start(bf16[16,4096]{1,0:T(8,128)(2,1)S(1)} %collective-permute-done.3.refs_5_.refs_13_), channel_id=1, source_target_pairs={{0,4},{1,5},{4,8},{5,9},{8,12},{9,13},{12,14},{13,15},{14,10},{15,... | collective-permute-start | bytes 393224 | tf_op jit(solution)/shard_map/ppermute | solution.py:399
  26.7 5.0 %collective-permute-start.7 = (bf16[16,4096]{1,0:T(8,128)(2,1)S(1)}, bf16[16,4096]{1,0:T(8,128)(2,1)S(1)}, u32[]{:S(2)}, u32[]{:S(2)}) collective-permute-start(bf16[16,4096]{1,0:T(8,128)(2,1)S(1)} %collective-permute-done.5.refs_7_.refs_15_), channel_id=1, source_target_pairs={{0,4},{1,5},{4,8},{5,9},{8,12},{9,13},{12,14},{13,15},{14,10},{15,... | collective-permute-start | bytes 393224 | tf_op jit(solution)/shard_map/ppermute | solution.py:399
  37.3 8.4 %collective-permute-start.9 = (bf16[528,128]{1,0:T(8,128)(2,1)}, bf16[528,128]{1,0:T(8,128)(2,1)S(1)}, u32[]{:S(2)}, u32[]{:S(2)}) collective-permute-start(bf16[528,128]{1,0:T(8,128)(2,1)} %attend.9), channel_id=1, source_target_pairs={{0,4},{1,5},{4,8},{5,9},{8,12},{9,13},{12,14},{13,15},{14,10},{15,... | collective-permute-start | bytes 405512 | tf_op jit(solution)/shard_map/ppermute | solution.py:432
  44.0 10.7 %collective-permute-start.11 = (bf16[528,128]{1,0:T(8,128)(2,1)}, bf16[528,128]{1,0:T(8,128)(2,1)S(1)}, u32[]{:S(2)}, u32[]{:S(2)}) collective-permute-start(bf16[528,128]{1,0:T(8,128)(2,1)} %get-tuple-element.29), channel_id=1, source_target_pairs={{0,2},{1,3},{4,0},{5,1},{8,4},{9,5},{12,8},{13,9},{14,12},{15,13},... | collective-permute-start | bytes 405512 | tf_op jit(solution)/shard_map/ppermute | solution.py:434
  48.0 6.7 %collective-permute-start.10 = (bf16[528,128]{1,0:T(8,128)(2,1)}, bf16[528,128]{1,0:T(8,128)(2,1)S(1)}, u32[]{:S(2)}, u32[]{:S(2)}) collective-permute-start(bf16[528,128]{1,0:T(8,128)(2,1)} %merge.3), channel_id=1, source_target_pairs={{0,4},{1,5},{4,8},{5,9},{8,12},{9,13},{12,14},{13,15},{14,10},{15,... | collective-permute-start | bytes 405512 | tf_op jit(solution)/shard_map/ppermute | solution.py:432
  57.4 8.3 %collective-permute-start.12 = (bf16[528,128]{1,0:T(8,128)(2,1)}, bf16[528,128]{1,0:T(8,128)(2,1)S(1)}, u32[]{:S(2)}, u32[]{:S(2)}) collective-permute-start(bf16[528,128]{1,0:T(8,128)(2,1)} %get-tuple-element.30), channel_id=1, source_target_pairs={{0,4},{1,5},{4,8},{5,9},{8,12},{9,13},{12,14},{13,15},{14,10},{15,... | collective-permute-start | bytes 405512 | tf_op jit(solution)/shard_map/ppermute | solution.py:432
  59.1 6.6 %collective-permute-start.13 = (bf16[528,128]{1,0:T(8,128)(2,1)}, bf16[528,128]{1,0:T(8,128)(2,1)S(1)}, u32[]{:S(2)}, u32[]{:S(2)}) collective-permute-start(bf16[528,128]{1,0:T(8,128)(2,1)} %get-tuple-element.32), channel_id=1, source_target_pairs={{0,2},{1,3},{4,0},{5,1},{8,4},{9,5},{12,8},{13,9},{14,12},{15,13},... | collective-permute-start | bytes 405512 | tf_op jit(solution)/shard_map/ppermute | solution.py:434
  68.3 7.0 %collective-permute-start.14 = (bf16[528,128]{1,0:T(8,128)(2,1)}, bf16[528,128]{1,0:T(8,128)(2,1)S(1)}, u32[]{:S(2)}, u32[]{:S(2)}) collective-permute-start(bf16[528,128]{1,0:T(8,128)(2,1)} %get-tuple-element.33), channel_id=1, source_target_pairs={{0,4},{1,5},{4,8},{5,9},{8,12},{9,13},{12,14},{13,15},{14,10},{15,... | collective-permute-start | bytes 405512 | tf_op jit(solution)/shard_map/ppermute | solution.py:432
  70.0 5.3 %collective-permute-start.15 = (bf16[528,128]{1,0:T(8,128)(2,1)}, bf16[528,128]{1,0:T(8,128)(2,1)S(1)}, u32[]{:S(2)}, u32[]{:S(2)}) collective-permute-start(bf16[528,128]{1,0:T(8,128)(2,1)} %get-tuple-element.34), channel_id=1, source_target_pairs={{0,2},{1,3},{4,0},{5,1},{8,4},{9,5},{12,8},{13,9},{14,12},{15,13},... | collective-permute-start | bytes 405512 | tf_op jit(solution)/shard_map/ppermute | solution.py:434
  81.0 5.5 %collective-permute-start.16 = (bf16[64,4096]{1,0:T(8,128)(2,1)}, bf16[64,4096]{1,0:T(8,128)(2,1)S(1)}, u32[]{:S(2)}, u32[]{:S(2)}) collective-permute-start(bf16[64,4096]{1,0:T(8,128)(2,1)} %get-tuple-element.36), channel_id=1, source_target_pairs={{0,1},{1,0},{2,3},{3,2},{4,5},{5,4},{6,7},{7,6},{8,9},{9,8},{10,11... | collective-permute-start | bytes 1572872 | tf_op jit(solution)/shard_map/ppermute | solution.py:441
  86.5 5.2 %collective-permute-start.17 = (bf16[8,4096]{1,0:T(8,128)(2,1)S(1)}, bf16[8,4096]{1,0:T(8,128)(2,1)S(1)}, u32[]{:S(2)}, u32[]{:S(2)}) collective-permute-start(bf16[8,4096]{1,0:T(8,128)(2,1)S(1)} %get-tuple-element.41), channel_id=1, source_target_pairs={{0,4},{1,5},{4,8},{5,9},{8,12},{9,13},{12,14},{13,15},{14,10},{15,... | collective-permute-start | bytes 196616 | tf_op jit(solution)/shard_map/ppermute | solution.py:456
  88.2 13.7 %collective-permute-start.21 = (bf16[8,4096]{1,0:T(8,128)(2,1)S(1)}, bf16[8,4096]{1,0:T(8,128)(2,1)S(1)}, u32[]{:S(2)}, u32[]{:S(2)}) collective-permute-start(bf16[8,4096]{1,0:T(8,128)(2,1)S(1)} %get-tuple-element.42), channel_id=1, source_target_pairs={{0,2},{1,3},{4,0},{5,1},{8,4},{9,5},{12,8},{13,9},{14,12},{15,13},... | collective-permute-start | bytes 196616 | tf_op jit(solution)/shard_map/ppermute | solution.py:461
  91.3 12.8 %collective-permute-start.29 = (bf16[8,4096]{1,0:T(8,128)(2,1)S(1)}, bf16[8,4096]{1,0:T(8,128)(2,1)S(1)}, u32[]{:S(2)}, u32[]{:S(2)}) collective-permute-start(bf16[8,4096]{1,0:T(8,128)(2,1)S(1)} %get-tuple-element.46), channel_id=1, source_target_pairs={{0,2},{1,3},{4,0},{5,1},{8,4},{9,5},{12,8},{13,9},{14,12},{15,13},... | collective-permute-start | bytes 196616 | tf_op jit(solution)/shard_map/ppermute | solution.py:461
  91.7 5.0 %collective-permute-start.18 = (bf16[8,4096]{1,0:T(8,128)(2,1)S(1)}, bf16[8,4096]{1,0:T(8,128)(2,1)S(1)}, u32[]{:S(2)}, u32[]{:S(2)}) collective-permute-start(bf16[8,4096]{1,0:T(8,128)(2,1)S(1)} %fusion.10), channel_id=1, source_target_pairs={{0,4},{1,5},{4,8},{5,9},{8,12},{9,13},{12,14},{13,15},{14,10},{15,... | collective-permute-start | bytes 196616 | tf_op jit(solution)/shard_map/ppermute | solution.py:456
  96.7 5.2 %collective-permute-start.19 = (bf16[8,4096]{1,0:T(8,128)(2,1)S(1)}, bf16[8,4096]{1,0:T(8,128)(2,1)S(1)}, u32[]{:S(2)}, u32[]{:S(2)}) collective-permute-start(bf16[8,4096]{1,0:T(8,128)(2,1)S(1)} %fusion.11), channel_id=1, source_target_pairs={{0,4},{1,5},{4,8},{5,9},{8,12},{9,13},{12,14},{13,15},{14,10},{15,... | collective-permute-start | bytes 196616 | tf_op jit(solution)/shard_map/ppermute | solution.py:456
  102.0 5.6 %collective-permute-start.22 = (bf16[8,4096]{1,0:T(8,128)(2,1)S(1)}, bf16[8,4096]{1,0:T(8,128)(2,1)S(1)}, u32[]{:S(2)}, u32[]{:S(2)}) collective-permute-start(bf16[8,4096]{1,0:T(8,128)(2,1)S(1)} %get-tuple-element.40), channel_id=1, source_target_pairs={{0,2},{1,3},{4,0},{5,1},{8,4},{9,5},{12,8},{13,9},{14,12},{15,13},... | collective-permute-start | bytes 196616 | tf_op jit(solution)/shard_map/ppermute | solution.py:461
  102.4 10.8 %collective-permute-start.20 = (bf16[8,4096]{1,0:T(8,128)(2,1)S(1)}, bf16[8,4096]{1,0:T(8,128)(2,1)S(1)}, u32[]{:S(2)}, u32[]{:S(2)}) collective-permute-start(bf16[8,4096]{1,0:T(8,128)(2,1)S(1)} %get-tuple-element.39), channel_id=1, source_target_pairs={{0,4},{1,5},{4,8},{5,9},{8,12},{9,13},{12,14},{13,15},{14,10},{15,... | collective-permute-start | bytes 196616 | tf_op jit(solution)/shard_map/ppermute | solution.py:456
  107.2 6.0 %collective-permute-start.28 = (bf16[8,4096]{1,0:T(8,128)(2,1)S(1)}, bf16[8,4096]{1,0:T(8,128)(2,1)S(1)}, u32[]{:S(2)}, u32[]{:S(2)}) collective-permute-start(bf16[8,4096]{1,0:T(8,128)(2,1)S(1)} %get-tuple-element.43), channel_id=1, source_target_pairs={{0,4},{1,5},{4,8},{5,9},{8,12},{9,13},{12,14},{13,15},{14,10},{15,... | collective-permute-start | bytes 196616 | tf_op jit(solution)/shard_map/ppermute | solution.py:456
  107.6 5.5 %collective-permute-start.23 = (bf16[8,4096]{1,0:T(8,128)(2,1)S(1)}, bf16[8,4096]{1,0:T(8,128)(2,1)S(1)}, u32[]{:S(2)}, u32[]{:S(2)}) collective-permute-start(bf16[8,4096]{1,0:T(8,128)(2,1)S(1)} %fusion.9), channel_id=1, source_target_pairs={{0,2},{1,3},{4,0},{5,1},{8,4},{9,5},{12,8},{13,9},{14,12},{15,13},... | collective-permute-start | bytes 196616 | tf_op jit(solution)/shard_map/ppermute | solution.py:461
  (26 other events, 131.6 us)

commit v3 on v2

--- a/solution.py
+++ b/solution.py
@@ -114,7 +114,8 @@
 NONE = -(2.0**100)
 LOG2E = 1.4426950408889634
 STAT_ROWS = 16
-ATTEND_VMEM = 60 * 1024 * 1024
+ATTEND_VMEM = 16 * 1024 * 1024
+SMALL_VMEM = 4 * 1024 * 1024
 
 
 def pack_stats(peaks, totals):
@@ -129,39 +130,52 @@
     return stats[:heads], stats[heads : 2 * heads] + stats[2 * heads : 3 * heads]
 
 
-def attend_kernel(heads, tile, order, groups, *refs):
-    n_blocks, count = order.shape[0], groups.shape[0]
-    q_blocks = refs[: n_blocks * count]
-    sources = refs[n_blocks * count : n_blocks * count + 2]
-    keep = refs[n_blocks * count + 2]
-    outs = refs[n_blocks * count + 3 : n_blocks * count + 3 + count]
-    held, q_all, scores, acc, arrived = refs[n_blocks * count + 3 + count :]
+def ring_chip(position, chips):
+    return jnp.where(position < chips // 2, 2 * position, 2 * (chips - 1 - position) + 1)
+
+
+def ring_place(chip, chips):
+    return jnp.where(chip % 2 == 0, chip // 2, chips - 1 - chip // 2)
+
+
+def near_chip(place, offset, chips):
+    position = place + (offset + chips) % chips
+    return ring_chip(jnp.where(position >= chips, position - chips, position), chips)
+
+
+def attend_kernel(heads, tile, offsets, targets, *refs):
+    n_blocks, count = len(offsets), len(targets)
+    q_blocks = refs[:n_blocks]
+    sources = refs[n_blocks : n_blocks + 2]
+    keep = refs[n_blocks + 2]
+    outs = refs[n_blocks + 3 : n_blocks + 3 + count]
+    q_all, scores, acc = refs[n_blocks + 3 + count :]
     block_rows = q_blocks[0].shape[0]
     rows = n_blocks * block_rows
     lanes = heads * rows
-    ctx = held.shape[1]
+    ctx = sources[0].shape[1]
     key_blocks, per_tile = ctx // BLOCK, tile // BLOCK
     to_log2 = HEAD ** (-0.5) * LOG2E
     units = [(i, s) for i in range(count) for s in range(2)]
-
-    def fetch(u, kind):
+    place = ring_place(lax.axis_index("ctx") // 2, n_blocks)
+    order = [near_chip(place, d, n_blocks) for d in offsets]
+    groups = [near_chip(place, d, n_blocks) for d in targets]
+
+    def load(u, kind, t):
         i, s = units[u]
         column = pl.ds(pl.multiple_of(groups[i] * HEAD, HEAD), HEAD)
-        at = 2 * u + kind
-        return pltpu.make_async_copy(sources[s].at[kind, :, column], held.at[at], arrived.at[at])
-
-    for u in range(len(units)):
-        for kind in range(2):
-            fetch(u, kind).start()
+        return sources[s][kind, t * tile : (t + 1) * tile, column]
+
     for i in range(count):
         for at in range(n_blocks):
             for h in range(heads):
-                q_all[i, h, order[at]] = q_blocks[i * n_blocks + at][:, h * HEAD : (h + 1) * HEAD]
+                column = pl.ds(pl.multiple_of((groups[i] * heads + h) * HEAD, HEAD), HEAD)
+                q_all[i, h, order[at]] = q_blocks[at][:, column]
 
     def score(u, t, peak):
         i, s = units[u]
         piece = lax.dot_general(
-            held[2 * u, t * tile : (t + 1) * tile, :],
+            load(u, 0, t),
             q_all[i].reshape(lanes, HEAD),
             (((1,), (1,)), ((), ())),
             preferred_element_type=jnp.float32,
@@ -185,7 +199,7 @@
             total = total + jnp.sum(weights.reshape(BLOCK // 8, 8, lanes), axis=0)
             probs.append(weights.astype(jnp.bfloat16))
         fresh = jnp.dot(
-            held[2 * u + 1, t * tile : (t + 1) * tile, :].T,
+            load(u, 1, t).T,
             jnp.concatenate(probs, axis=0),
             preferred_element_type=jnp.float32,
         )
@@ -194,7 +208,6 @@
 
     tiles = range(ctx // tile)
     lowest = jnp.full((8, lanes), NONE, jnp.float32)
-    fetch(0, 0).wait()
     peak = lowest
     for t in tiles:
         peak = score(0, t, peak)
@@ -202,10 +215,7 @@
     for u, (i, s) in enumerate(units):
         row = jnp.max(peak, axis=0, keepdims=True)
         total = jnp.zeros((8, lanes), jnp.float32)
-        fetch(u, 1).wait()
         peak = lowest
-        if u + 1 < len(units):
-            fetch(u + 1, 0).wait()
         for t in tiles:
             if u + 1 < len(units):
                 peak = score(u + 1, t, peak)
@@ -225,46 +235,36 @@
             )
 
 
-def attend(q_blocks, order, groups, kv, kv_far, keep, heads, tile=256):
-    count = groups.shape[0]
-    n_blocks = len(q_blocks)
+def in_vmem(x):
+    return pltpu.with_memory_space_constraint(x, pltpu.VMEM)
+
+
+def attend(q_blocks, offsets, targets, kv, kv_far, keep, heads, tile=256):
+    count, n_blocks = len(targets), len(q_blocks)
     block_rows = q_blocks[0].shape[0]
     rows = block_rows * n_blocks
     ctx = kv.shape[1]
     width = heads * HEAD
     length = width + STAT_ROWS
+    whole = pl.BlockSpec(memory_space=pltpu.VMEM)
     return pl.pallas_call(
-        lambda *refs: attend_kernel(heads, tile, *refs),
-        grid_spec=pltpu.PrefetchScalarGridSpec(
-            num_scalar_prefetch=2,
-            grid=(1,),
-            in_specs=[
-                pl.BlockSpec((block_rows, width), lambda z, o, g, i=i: (0, g[i]))
-                for i in range(count)
-                for _ in q_blocks
-            ]
-            + [pl.BlockSpec(memory_space=pl.ANY)] * 2
-            + [pl.BlockSpec(keep.shape, lambda z, o, g: (0, 0))],
-            out_specs=[pl.BlockSpec((length, rows), lambda z, o, g: (0, 0)) for _ in range(count)],
-            scratch_shapes=[
-                pltpu.VMEM((4 * count, ctx, HEAD), jnp.bfloat16),
-                pltpu.VMEM((count, heads, n_blocks, block_rows, HEAD), jnp.bfloat16),
-                pltpu.VMEM((2, ctx, heads * rows), jnp.float32),
-                pltpu.VMEM((2, HEAD, heads * rows), jnp.float32),
-                pltpu.SemaphoreType.DMA((4 * count,)),
-            ],
-        ),
-        out_shape=[jax.ShapeDtypeStruct((length, rows), jnp.bfloat16) for _ in range(count)],
-        compiler_params=pltpu.CompilerParams(
-            dimension_semantics=("arbitrary",), vmem_limit_bytes=ATTEND_VMEM
-        ),
+        lambda *refs: attend_kernel(heads, tile, offsets, targets, *refs),
+        in_specs=[whole] * (n_blocks + 3),
+        out_specs=[whole] * count,
+        scratch_shapes=[
+            pltpu.VMEM((count, heads, n_blocks, block_rows, HEAD), jnp.bfloat16),
+            pltpu.VMEM((2, ctx, heads * rows), jnp.float32),
+            pltpu.VMEM((2, HEAD, heads * rows), jnp.float32),
+        ],
+        out_shape=[pltpu.VMEM((length, rows), jnp.bfloat16) for _ in range(count)],
+        compiler_params=pltpu.CompilerParams(vmem_limit_bytes=ATTEND_VMEM),
         cost_estimate=pl.CostEstimate(
             flops=12 * count * rows * width * 2 * ctx,
             bytes_accessed=8 * count * ctx * HEAD,
             transcendentals=count * rows * heads * 2 * ctx,
         ),
         name="attend",
-    )(order, groups, *(list(q_blocks) * count), kv, kv_far, keep)
+    )(*[in_vmem(x) for x in q_blocks], in_vmem(kv), in_vmem(kv_far), in_vmem(keep))
 
 
 def merge_parts(parts, heads):
@@ -295,69 +295,135 @@
 
 def merge(pairs, heads):
     shape = pairs[0][0].shape
-    spec = pl.BlockSpec(shape, lambda: (0, 0))
+    whole = pl.BlockSpec(memory_space=pltpu.VMEM)
     return pl.pallas_call(
         lambda *refs: merge_kernel(heads, len(pairs), *refs),
-        in_specs=[spec] * (2 * len(pairs)),
-        out_specs=[spec] * len(pairs),
-        out_shape=[jax.ShapeDtypeStruct(shape, jnp.bfloat16)] * len(pairs),
-        compiler_params=pltpu.CompilerParams(vmem_limit_bytes=ATTEND_VMEM),
+        in_specs=[whole] * (2 * len(pairs)),
+        out_specs=[whole] * len(pairs),
+        out_shape=[pltpu.VMEM(shape, jnp.bfloat16)] * len(pairs),
+        compiler_params=pltpu.CompilerParams(vmem_limit_bytes=SMALL_VMEM),
         cost_estimate=pl.CostEstimate(
             flops=1000000, bytes_accessed=6 * shape[0] * shape[1] * len(pairs), transcendentals=0
         ),
         name="merge",
-    )(*[x for pair in pairs for x in pair])
-
-
-def project_kernel(heads, core, *refs):
-    parts, (w_ref, kept, sent, attended) = refs[:-4], refs[-4:]
-
-    @pl.when(pl.program_id(0) == 0)
-    def _():
-        _, total, values = merge_parts(parts, heads)
-        for h in range(heads):
-            mean = values[h] / total[h : h + 1]
-            attended[:, h * HEAD : (h + 1) * HEAD] = mean.T.astype(jnp.bfloat16)
-
-    full = jnp.dot(attended[...], w_ref[...], preferred_element_type=jnp.float32)
-    chips, per_dev, tile = kept.shape
-    full = full.reshape(chips, 2, per_dev, tile)
-    first = core[0] == 0
-    kept[...] = jnp.where(first, full[:, 0], full[:, 1])
-    away = jnp.where(first, full[:, 1], full[:, 0])
-    sent[...] = away.reshape(chips * per_dev, tile).astype(jnp.bfloat16)
-
-
-def project(parts, core, w_out, heads, per_dev, part, part_count, tile=1024):
+    )(*[in_vmem(x) for pair in pairs for x in pair])
+
+
+def finish_kernel(heads, *refs):
+    parts, attended = refs[:-1], refs[-1]
+    _, total, values = merge_parts(parts, heads)
+    for h in range(heads):
+        mean = values[h] / total[h : h + 1]
+        attended[:, h * HEAD : (h + 1) * HEAD] = mean.T.astype(jnp.bfloat16)
+
+
+def finish(parts, heads):
     length, rows = parts[0].shape
+    whole = pl.BlockSpec(memory_space=pltpu.VMEM)
+    return pl.pallas_call(
+        lambda *refs: finish_kernel(heads, *refs),
+        in_specs=[whole] * len(parts),
+        out_specs=whole,
+        out_shape=pltpu.VMEM((rows, heads * HEAD), jnp.bfloat16),
+        compiler_params=pltpu.CompilerParams(vmem_limit_bytes=SMALL_VMEM),
+        cost_estimate=pl.CostEstimate(
+            flops=1000000, bytes_accessed=2 * length * rows * len(parts), transcendentals=0
+        ),
+        name="finish",
+    )(*[in_vmem(x) for x in parts])
+
+
+def project_kernel(low, tile, attended, w_ref, kept, sent):
+    chips, per_dev, cols = kept.shape
+    first = lax.axis_index("ctx") % 2 == 0
+    for j in range(cols // tile):
+        span = slice(j * tile, (j + 1) * tile)
+        full = jnp.dot(
+            attended[...],
+            w_ref[:, low + j * tile : low + (j + 1) * tile],
+            preferred_element_type=jnp.float32,
+        )
+        full = full.reshape(chips, 2, per_dev, tile)
+        kept[:, :, span] = jnp.where(first, full[:, 0], full[:, 1])
+        away = jnp.where(first, full[:, 1], full[:, 0])
+        sent[:, :, span] = away.astype(jnp.bfloat16)
+
+
+def project(attended, w_out, per_dev, part, part_count, tile=512):
+    rows, width = attended.shape
     chips = rows // (2 * per_dev)
     cols = w_out.shape[1] // part_count
-    steps = cols // tile
+    whole = pl.BlockSpec(memory_space=pltpu.VMEM)
     return pl.pallas_call(
-        lambda *refs: project_kernel(heads, *refs),
-        grid_spec=pltpu.PrefetchScalarGridSpec(
-            num_scalar_prefetch=1,
-            grid=(steps,),
-            in_specs=[pl.BlockSpec((length, rows), lambda j, c: (0, 0)) for _ in parts]
-            + [pl.BlockSpec((heads * HEAD, tile), lambda j, c: (0, j + part * steps))],
-            out_specs=[
-                pl.BlockSpec((chips, per_dev, tile), lambda j, c: (0, 0, j)),
-                pl.BlockSpec((chips * per_dev, tile), lambda j, c: (0, j)),
-            ],
-            scratch_shapes=[pltpu.VMEM((rows, heads * HEAD), jnp.bfloat16)],
-        ),
+        lambda *refs: project_kernel(part * cols, tile, *refs),
+        in_specs=[whole] * 2,
+        out_specs=[whole] * 2,
         out_shape=[
-            jax.ShapeDtypeStruct((chips, per_dev, cols), jnp.float32),
-            jax.ShapeDtypeStruct((chips * per_dev, cols), jnp.bfloat16),
+            pltpu.VMEM((chips, per_dev, cols), jnp.float32),
+            pltpu.VMEM((chips, per_dev, cols), jnp.bfloat16),
         ],
-        compiler_params=pltpu.CompilerParams(dimension_semantics=("arbitrary",)),
+        compiler_params=pltpu.CompilerParams(vmem_limit_bytes=SMALL_VMEM),
         cost_estimate=pl.CostEstimate(
-            flops=2 * rows * heads * HEAD * cols,
-            bytes_accessed=3 * heads * HEAD * cols,
-            transcendentals=0,
+            flops=2 * rows * width * cols, bytes_accessed=3 * width * cols, transcendentals=0
         ),
         name="project",
-    )(core, *parts, w_out)
+    )(in_vmem(attended), in_vmem(w_out))
+
+
+def fold_kernel(targets, pieces, refs_per, *refs):
+    terms = refs[: 2 * pieces]
+    came = refs[2 * pieces : len(refs) - len(targets)]
+    outs = refs[len(refs) - len(targets) :]
+    chips, _, cols = terms[0].shape
+    place = ring_place(lax.axis_index("ctx") // 2, chips)
+    for i, target in enumerate(targets):
+        chip = near_chip(place, target, chips)
+        mine = came[i * refs_per : (i + 1) * refs_per]
+        for h in range(pieces):
+            span = slice(h * cols, (h + 1) * cols)
+            total = terms[2 * h][chip] + terms[2 * h + 1][chip].astype(jnp.float32)
+            for ref in mine:
+                total = total + ref[:, span].astype(jnp.float32)
+            outs[i][:, span] = total.astype(jnp.bfloat16)
+
+
+def fold(targets, terms, came, last=False):
+    _, per_dev, cols = terms[0].shape
+    shape = (per_dev, cols * len(terms) // 2)
+    whole = pl.BlockSpec(memory_space=pltpu.VMEM)
+    made = jax.ShapeDtypeStruct(shape, jnp.bfloat16) if last else pltpu.VMEM(shape, jnp.bfloat16)
+    return pl.pallas_call(
+        lambda *refs: fold_kernel(targets, len(terms) // 2, len(came) // len(targets), *refs),
+        in_specs=[whole] * (len(terms) + len(came)),
+        out_specs=[whole] * len(targets),
+        out_shape=[made] * len(targets),
+        compiler_params=pltpu.CompilerParams(vmem_limit_bytes=SMALL_VMEM),
+        cost_estimate=pl.CostEstimate(
+            flops=1000000, bytes_accessed=20 * per_dev * cols * len(targets), transcendentals=0
+        ),
+        name="fold",
+    )(*[in_vmem(x) for x in list(terms) + list(came)])
+
+
+def stage_kernel(source, held, done):
+    copy = pltpu.make_async_copy(source, held, done)
+    copy.start()
+    copy.wait()
+
+
+def stage(x):
+    return pl.pallas_call(
+        stage_kernel,
+        in_specs=[pl.BlockSpec(memory_space=pl.ANY)],
+        out_specs=pl.BlockSpec(memory_space=pltpu.VMEM),
+        out_shape=pltpu.VMEM(x.shape, x.dtype),
+        scratch_shapes=[pltpu.SemaphoreType.DMA],
+        compiler_params=pltpu.CompilerParams(vmem_limit_bytes=SMALL_VMEM),
+        cost_estimate=pl.CostEstimate(
+            flops=0, bytes_accessed=2 * x.size * x.dtype.itemsize, transcendentals=0
+        ),
+        name="stage",
+    )(x)
 
 
 def paired_device(queries, steer_ids, steer_table, kv, blocks, w_out):
@@ -379,12 +445,6 @@
         ]
 
     ahead_pairs, behind_pairs = hop(1), hop(-1)
-    place = jnp.where(chip % 2 == 0, chip // 2, chips - 1 - chip // 2)
-
-    def chip_at(offset):
-        p = (place + offset) % chips
-        return jnp.where(p < chips // 2, 2 * p, 2 * (chips - 1 - p) + 1)
-
     steered = apply_steer(queries, steer_ids, steer_table)
     halves = steered.reshape(per_dev, chips, 2, width)
     mine = jnp.where(core == 0, halves[:, :, 0], halves[:, :, 1]).reshape(per_dev, D // 2)
@@ -393,20 +453,21 @@
     block = jnp.concatenate(
         [jnp.where(core == 0, mine, theirs), jnp.where(core == 0, theirs, mine)], axis=0
     )
+    half = chips // 2
+    far_pairs = hop(half)
     found, offsets = [block], [0]
-    ahead, behind = block, block
-    for s in range(1, chips // 2 + 1):
+    ahead, behind, far = block, block, None
+    for s in range(1, half):
         ahead = lax.ppermute(ahead, "ctx", ahead_pairs)
-        found.append(ahead)
-        offsets.append(-s)
-        if s < chips - s:
-            behind = lax.ppermute(behind, "ctx", behind_pairs)
-            found.append(behind)
-            offsets.append(s)
+        behind = lax.ppermute(behind, "ctx", behind_pairs)
         if s == 1:
+            far = lax.ppermute(block, "ctx", far_pairs)
             ahead, kv_late, blocks_late = lax.optimization_barrier((ahead, kv, blocks))
             kv_far = lax.ppermute(kv_late, "ctx", swap)
-    order = chip_at(jnp.array(offsets, jnp.int32))
+        found += [ahead, behind]
+        offsets += [-s, s]
+    found.append(far)
+    offsets.append(half)
 
     block_count = kv.shape[1] // BLOCK
     ids = jnp.arange(2 * block_count, dtype=jnp.int32)
@@ -415,55 +476,40 @@
     keep = jnp.repeat(hits.T.astype(jnp.float32), BLOCK, axis=1)
     keep = jnp.concatenate([keep] * heads, axis=1)
 
-    half = chips // 2
+    kv_near = stage(kv_late)
 
     def attend_for(targets):
-        groups = chip_at(jnp.array(targets, jnp.int32))
-        return attend(found, order, groups, kv, kv_far, keep, heads)
-
-    went_ahead, went_behind = None, None
-    for s in range(1, half + 1):
-        outs = attend_for([half + 1 - s] + ([s - 1 - half] if s > 1 else []))
-        came = [went_ahead, went_behind]
-        pairs = [(x, y) for x, y in zip(outs, came) if y is not None]
-        if pairs:
-            merged = merge(pairs, heads)
-            outs = list(merged) + list(outs[len(merged) :])
+        return attend(found, offsets, targets, kv_near, kv_far, keep, heads)
+
+    went_ahead, went_behind, went_far = None, None, None
+    for s in range(1, half):
+        targets = [half - s, s - half]
+        if s == 1:
+            outs = attend_for(targets + [half])
+            last = outs[2]
+        else:
+            outs = merge(list(zip(attend_for(targets), [went_ahead, went_behind])), heads)
         went_ahead = lax.ppermute(outs[0], "ctx", ahead_pairs)
-        if s > 1:
-            went_behind = lax.ppermute(outs[1], "ctx", behind_pairs)
-    parts = [attend_for([0])[0], went_ahead, went_behind]
-
+        went_behind = lax.ppermute(outs[1], "ctx", behind_pairs)
+        if s == 1:
+            went_far = lax.ppermute(last, "ctx", far_pairs)
+    parts = [attend_for([0])[0], went_ahead, went_behind, went_far]
+
+    attended = finish(parts, heads)
     col_parts = 2
-    pieces = []
+    terms = []
     for h in range(col_parts):
-        kept, sent = project(parts, core.reshape(1), w_out, heads, per_dev, h, col_parts)
-        got = lax.ppermute(sent, "ctx", swap).reshape(kept.shape)
-        pieces.append((kept, got))
-
-    def term(piece, offset):
-        at = chip_at(offset)
-        pick = [lax.dynamic_index_in_dim(x, at, 0, keepdims=False) for x in piece]
-        return pick[0] + pick[1].astype(jnp.float32)
-
-    streams = [[None, None] for _ in pieces]
-    for s in range(1, half + 1):
-        for h, piece in enumerate(pieces):
-            came_ahead, came_behind = streams[h]
-            total = term(piece, half + 1 - s)
-            if came_ahead is not None:
-                total = total + came_ahead.astype(jnp.float32)
-            streams[h][0] = lax.ppermute(total.astype(jnp.bfloat16), "ctx", ahead_pairs)
-            if s > 1:
-                total = term(piece, s - 1 - half)
-                if came_behind is not None:
-                    total = total + came_behind.astype(jnp.float32)
-                streams[h][1] = lax.ppermute(total.astype(jnp.bfloat16), "ctx", behind_pairs)
-    done = []
-    for piece, (came_ahead, came_behind) in zip(pieces, streams):
-        total = term(piece, 0) + came_ahead.astype(jnp.float32) + came_behind.astype(jnp.float32)
-        done.append(total.astype(jnp.bfloat16))
-    return jnp.concatenate(done, axis=1)
+        kept, sent = project(attended, w_out, per_dev, h, col_parts)
+        terms += [kept, lax.ppermute(sent, "ctx", swap)]
+    went_ahead, went_behind, went_far = None, None, None
+    for s in range(1, half):
+        came = [] if s == 1 else [went_ahead, went_behind]
+        outs = fold([half - s, s - half] + ([half] if s == 1 else []), terms, came)
+        went_ahead = lax.ppermute(outs[0], "ctx", ahead_pairs)
+        went_behind = lax.ppermute(outs[1], "ctx", behind_pairs)
+        if s == 1:
+            went_far = lax.ppermute(outs[2], "ctx", far_pairs)
+    return fold([0], terms, [went_ahead, went_behind, went_far], last=True)[0]
 
 
 def solution(mesh):

time: 118 us -> 88.4 us (0.75)
  Pallas kernels: 44.2 us -> 24.4 us
  other arithmetic: 11.2 us -> 0.91 us
  waiting for transfers between devices: 19.4 us -> 23.9 us
  starting transfers between devices: 35.8 us -> 34 us
    pallas_call x7 -> x12, Pallas kernels: 38.7 us -> 24.1 us  [the longest x4 21.2 us: attend(): pl.pallas_call(lambda *refs: attend_kernel(heads, tile, offsets, targets,...]
    ppermute x16 -> x5, starting transfers between devices: 19.6 us -> 9.42 us  [the longest x1 3.55 us: paired_device(): far = lax.ppermute(block, 'ctx', far_pairs)]
    ppermute x3, waiting for transfers between devices: 8.68 us -> 1.91 us  [paired_device(): behind = lax.ppermute(behind, 'ctx', behind_pairs)]
    ppermute x4 -> x6, waiting for transfers between devices: 0.01 us -> 6.43 us  [paired_device(): went_ahead = lax.ppermute(outs[0], 'ctx', ahead_pairs)]
    convert_element_type x12 -> x0, other arithmetic: 5.92 us -> none  [the longest x8 3.99 us: paired_device(): streams[h][0] = lax.ppermute(total.astype(jnp.bfloat16), 'ctx', ahead_pairs)]
    pallas_call x3 -> x2, Pallas kernels: 5.52 us -> 0.25 us  [merge(): pl.pallas_call(lambda *refs: merge_kernel(heads, len(pairs), *refs), in_s...]
    ppermute x4 -> x6, starting transfers between devices: 4.22 us -> 8.56 us  [paired_device(): went_ahead = lax.ppermute(outs[0], 'ctx', ahead_pairs)]
    ppermute x3 -> x6, starting transfers between devices: 2.36 us -> 6.38 us  [paired_device(): went_behind = lax.ppermute(outs[1], 'ctx', behind_pairs)]
  transfers between devices with their start and end apart: 32 -> 25, of which waited for: 11 -> 14; matrix products, arithmetic and copies ran while one was open for 8% -> 1% of each run, Pallas kernels for 26% -> 17%
where the time goes in v3:
time: 88.4 us; the launch traced here: 88.1 us
  starting transfers between devices  34 us (38%)
  Pallas kernels  24.4 us (28%)
  waiting for transfers between devices  23.9 us (27%)
  local copies, waits for them, and re-layouts  3.43 us (4%)
  matrix products  1.15 us (1%)
  other arithmetic  0.91 us (1%)
    pallas_call x4, Pallas kernels, attend(): pl.pallas_call(lambda *refs: attend_kernel(heads, tile, offsets, targets,...  21.2 us
    ppermute x3, waiting for transfers between devices, paired_device(): ahead = lax.ppermute(ahead, 'ctx', ahead_pairs)  8.58 us
    ppermute x6, starting transfers between devices, paired_device(): went_ahead = lax.ppermute(outs[0], 'ctx', ahead_pairs)  8.56 us
    ppermute x6, waiting for transfers between devices, paired_device(): went_ahead = lax.ppermute(outs[0], 'ctx', ahead_pairs)  6.43 us
    ppermute x6, starting transfers between devices, paired_device(): went_behind = lax.ppermute(outs[1], 'ctx', behind_pairs)  6.38 us
    ppermute x3, starting transfers between devices, paired_device(): ahead = lax.ppermute(ahead, 'ctx', ahead_pairs)  5.28 us
    ppermute x3, starting transfers between devices, paired_device(): behind = lax.ppermute(behind, 'ctx', behind_pairs)  3.85 us
    ppermute x6, waiting for transfers between devices, paired_device(): went_behind = lax.ppermute(outs[1], 'ctx', behind_pairs)  3.78 us
  transfers between devices with their start and end apart: 25, of which 14 were waited for; matrix products, arithmetic and copies ran while one was open for 1% of the time, Pallas kernels for 17%

profile of v3, /device:TPU:0, one launch (start us, length us, event | category | flops | bytes accessed | tf_op | source)
XLA Modules:
  0.0 88.1 jit_solution(1924192437141153149)
XLA Ops:
  3.6 3.0 %collective-permute-start.1 = (bf16[16,4096]{1,0:T(8,128)(2,1)S(1)}, bf16[16,4096]{1,0:T(8,128)(2,1)S(1)}, u32[]{:S(2)}, u32[]{:S(2)}) collective-permute-start(bf16[16,4096]{1,0:T(8,128)(2,1)S(1)} %pad_maximum_fusion.refs_0_), channel_id=1, source_target_pairs={{0,4},{1,5},{4,8},{5,9},{8,12},{9,13},{12,14},{13,15},{14,10},{15,... | collective-permute-start | bytes 393224 | tf_op jit(solution)/shard_map/ppermute | solution.py:461
  6.6 3.8 %collective-permute-done.1.refs_1_ = bf16[16,4096]{1,0:T(8,128)(2,1)S(1)} collective-permute-done((bf16[16,4096]{1,0:T(8,128)(2,1)S(1)}, bf16[16,4096]{1,0:T(8,128)(2,1)S(1)}, u32[]{:S(2)}, u32[]{:S(2)}) %collective-permute-start.1) | collective-permute-done | bytes 131104 | tf_op jit(solution)/shard_map/ppermute | solution.py:461
  10.4 1.8 %collective-permute-start.2 = (bf16[16,4096]{1,0:T(8,128)(2,1)S(1)}, bf16[16,4096]{1,0:T(8,128)(2,1)S(1)}, u32[]{:S(2)}, u32[]{:S(2)}) collective-permute-start(bf16[16,4096]{1,0:T(8,128)(2,1)S(1)} %pad_maximum_fusion.refs_0_), channel_id=1, source_target_pairs={{0,2},{1,3},{4,0},{5,1},{8,4},{9,5},{12,8},{13,9},{14,12},{15,13},... | collective-permute-start | bytes 393224 | tf_op jit(solution)/shard_map/ppermute | solution.py:462
  12.1 3.5 %collective-permute-start.7 = (bf16[16,4096]{1,0:T(8,128)(2,1)S(1)}, bf16[16,4096]{1,0:T(8,128)(2,1)S(1)}, u32[]{:S(2)}, u32[]{:S(2)}) collective-permute-start(bf16[16,4096]{1,0:T(8,128)(2,1)S(1)} %pad_maximum_fusion.refs_0_), channel_id=1, source_target_pairs={{0,14},{1,15},{4,10},{5,11},{8,6},{9,7},{12,2},{13,3},{14,0},{15,1... | collective-permute-start | bytes 393224 | tf_op jit(solution)/shard_map/ppermute | solution.py:464
  17.5 1.4 %collective-permute-start.4 = (bf16[16,4096]{1,0:T(8,128)(2,1)S(1)}, bf16[16,4096]{1,0:T(8,128)(2,1)S(1)}, u32[]{:S(2)}, u32[]{:S(2)}) collective-permute-start(bf16[16,4096]{1,0:T(8,128)(2,1)S(1)} %collective-permute-done.2.refs_2_), channel_id=1, source_target_pairs={{0,2},{1,3},{4,0},{5,1},{8,4},{9,5},{12,8},{13,9},{14,12},{15,13},... | collective-permute-start | bytes 393224 | tf_op jit(solution)/shard_map/ppermute | solution.py:462
  18.9 4.5 %collective-permute-done.3.refs_3_ = bf16[16,4096]{1,0:T(8,128)(2,1)S(1)} collective-permute-done((bf16[16,4096]{1,0:T(8,128)(2,1)S(1)}, bf16[16,4096]{1,0:T(8,128)(2,1)S(1)}, u32[]{:S(2)}, u32[]{:S(2)}) %collective-permute-start.3) | collective-permute-done | bytes 131104 | tf_op jit(solution)/shard_map/ppermute | solution.py:461
  23.3 1.7 %collective-permute-start.5 = (bf16[16,4096]{1,0:T(8,128)(2,1)S(1)}, bf16[16,4096]{1,0:T(8,128)(2,1)S(1)}, u32[]{:S(2)}, u32[]{:S(2)}) collective-permute-start(bf16[16,4096]{1,0:T(8,128)(2,1)S(1)} %collective-permute-done.3.refs_3_), channel_id=1, source_target_pairs={{0,4},{1,5},{4,8},{5,9},{8,12},{9,13},{12,14},{13,15},{14,10},{15,... | collective-permute-start | bytes 393224 | tf_op jit(solution)/shard_map/ppermute | solution.py:461
  25.7 2.2 %copy-done.1 = bf16[2,1024,1024]{2,1,0:T(8,128)(2,1)S(1)} copy-done((bf16[2,1024,1024]{2,1,0:T(8,128)(2,1)S(1)}, bf16[2,1024,1024]{2,1,0:T(8,128)(2,1)}, u32[]{:S(2)}) %copy-start.1) | copy-done | bytes 4194328
  28.6 1.9 %collective-permute-done.6.refs_6_ = bf16[16,4096]{1,0:T(8,128)(2,1)S(1)} collective-permute-done((bf16[16,4096]{1,0:T(8,128)(2,1)S(1)}, bf16[16,4096]{1,0:T(8,128)(2,1)S(1)}, u32[]{:S(2)}, u32[]{:S(2)}) %collective-permute-start.6) | collective-permute-done | bytes 131104 | tf_op jit(solution)/shard_map/ppermute | solution.py:462
  30.5 6.6 %attend.7 = (bf16[528,128]{1,0:T(8,128)(2,1)S(1)}, bf16[528,128]{1,0:T(8,128)(2,1)S(1)}, bf16[528,128]{1,0:T(8,128)(2,1)S(1)}) custom-call(bf16[16,4096]{1,0:T(8,128)(2,1)S(1)} %pad_maximum_fusion.refs_0_, bf16[16,4096]{1,0:T(8,128)(2,1)S(1)} %collective-permute-done.1.refs_1_, bf16[16,4096]{1,0:T(8,128)(2,1)S(1)} %collective-permute-done.2.refs_2_, ...), custom_call_target="tpu_custom_call" | custom-call | flops 4831838208 | bytes 3145728 | tf_op jit(solution)/shard_map/attend/pallas_call | solution.py:250
  37.8 1.4 %collective-permute-start.9 = (bf16[528,128]{1,0:T(8,128)(2,1)S(1)}, bf16[528,128]{1,0:T(8,128)(2,1)S(1)}, u32[]{:S(2)}, u32[]{:S(2)}) collective-permute-start(bf16[528,128]{1,0:T(8,128)(2,1)S(1)} %get-tuple-element.35), channel_id=1, source_target_pairs={{0,4},{1,5},{4,8},{5,9},{8,12},{9,13},{12,14},{13,15},{14,10},{15,... | collective-permute-start | bytes 405512 | tf_op jit(solution)/shard_map/ppermute | solution.py:492
  39.2 2.9 %collective-permute-start.15 = (bf16[528,128]{1,0:T(8,128)(2,1)S(1)}, bf16[528,128]{1,0:T(8,128)(2,1)S(1)}, u32[]{:S(2)}, u32[]{:S(2)}) collective-permute-start(bf16[528,128]{1,0:T(8,128)(2,1)S(1)} %get-tuple-element.43), channel_id=1, source_target_pairs={{0,14},{1,15},{4,10},{5,11},{8,6},{9,7},{12,2},{13,3},{14,0},{15,1... | collective-permute-start | bytes 405512 | tf_op jit(solution)/shard_map/ppermute | solution.py:495
  42.2 5.4 %attend.6 = (bf16[528,128]{1,0:T(8,128)(2,1)S(1)}, bf16[528,128]{1,0:T(8,128)(2,1)S(1)}) custom-call(bf16[16,4096]{1,0:T(8,128)(2,1)S(1)} %pad_maximum_fusion.refs_0_, bf16[16,4096]{1,0:T(8,128)(2,1)S(1)} %collective-permute-done.1.refs_1_, bf16[16,4096]{1,0:T(8,128)(2,1)S(1)} %collective-permute-done.2.refs_2_, ...), custom_call_target="tpu_custom_call" | custom-call | flops 3221225472 | bytes 2097152 | tf_op jit(solution)/shard_map/attend/pallas_call | solution.py:250
  48.3 1.6 %collective-permute-start.12 = (bf16[528,128]{1,0:T(8,128)(2,1)S(1)}, bf16[528,128]{1,0:T(8,128)(2,1)S(1)}, u32[]{:S(2)}, u32[]{:S(2)}) collective-permute-start(bf16[528,128]{1,0:T(8,128)(2,1)S(1)} %get-tuple-element.40), channel_id=1, source_target_pairs={{0,2},{1,3},{4,0},{5,1},{8,4},{9,5},{12,8},{13,9},{14,12},{15,13},... | collective-permute-start | bytes 405512 | tf_op jit(solution)/shard_map/ppermute | solution.py:493
  49.8 5.2 %attend.5 = (bf16[528,128]{1,0:T(8,128)(2,1)S(1)}, bf16[528,128]{1,0:T(8,128)(2,1)S(1)}) custom-call(bf16[16,4096]{1,0:T(8,128)(2,1)S(1)} %pad_maximum_fusion.refs_0_, bf16[16,4096]{1,0:T(8,128)(2,1)S(1)} %collective-permute-done.1.refs_1_, bf16[16,4096]{1,0:T(8,128)(2,1)S(1)} %collective-permute-done.2.refs_2_, ...), custom_call_target="tpu_custom_call" | custom-call | flops 3221225472 | bytes 2097152 | tf_op jit(solution)/shard_map/attend/pallas_call | solution.py:250
  55.8 1.5 %collective-permute-start.14 = (bf16[528,128]{1,0:T(8,128)(2,1)S(1)}, bf16[528,128]{1,0:T(8,128)(2,1)S(1)}, u32[]{:S(2)}, u32[]{:S(2)}) collective-permute-start(bf16[528,128]{1,0:T(8,128)(2,1)S(1)} %get-tuple-element.42), channel_id=1, source_target_pairs={{0,2},{1,3},{4,0},{5,1},{8,4},{9,5},{12,8},{13,9},{14,12},{15,13},... | collective-permute-start | bytes 405512 | tf_op jit(solution)/shard_map/ppermute | solution.py:493
  57.3 3.9 %attend.4.refs_0_ = bf16[528,128]{1,0:T(8,128)(2,1)S(1)} custom-call(bf16[16,4096]{1,0:T(8,128)(2,1)S(1)} %pad_maximum_fusion.refs_0_, bf16[16,4096]{1,0:T(8,128)(2,1)S(1)} %collective-permute-done.1.refs_1_, bf16[16,4096]{1,0:T(8,128)(2,1)S(1)} %collective-permute-done.2.refs_2_, bf16[16,4096]{1,0:T(8,128)(2,1)S(1)} %collective-permute-done.3.refs_3_, ...), custom_call_target="tpu_custom_call" | custom-call | flops 1610612736 | bytes 1048576 | tf_op jit(solution)/shard_map/attend/pallas_call | solution.py:250
  63.5 1.4 %collective-permute-done.16.refs_1_ = bf16[8,8,4096]{2,1,0:T(8,128)(2,1)S(1)} collective-permute-done((bf16[8,8,4096]{2,1,0:T(8,128)(2,1)S(1)}, bf16[8,8,4096]{2,1,0:T(8,128)(2,1)S(1)}, u32[]{:S(2)}, u32[]{:S(2)}) %collective-permute-start.16) | collective-permute-done | bytes 524320 | tf_op jit(solution)/shard_map/ppermute | solution.py:503
  66.3 1.5 %collective-permute-start.19 = (bf16[8,8192]{1,0:T(8,128)(2,1)S(1)}, bf16[8,8192]{1,0:T(8,128)(2,1)S(1)}, u32[]{:S(2)}, u32[]{:S(2)}) collective-permute-start(bf16[8,8192]{1,0:T(8,128)(2,1)S(1)} %get-tuple-element.49), channel_id=1, source_target_pairs={{0,2},{1,3},{4,0},{5,1},{8,4},{9,5},{12,8},{13,9},{14,12},{15,13},... | collective-permute-start | bytes 393224 | tf_op jit(solution)/shard_map/ppermute | solution.py:509
  67.8 3.5 %collective-permute-done.18.refs_4_ = bf16[8,8192]{1,0:T(8,128)(2,1)S(1)} collective-permute-done((bf16[8,8192]{1,0:T(8,128)(2,1)S(1)}, bf16[8,8192]{1,0:T(8,128)(2,1)S(1)}, u32[]{:S(2)}, u32[]{:S(2)}) %collective-permute-start.18) | collective-permute-done | bytes 131104 | tf_op jit(solution)/shard_map/ppermute | solution.py:508
  73.7 2.4 %collective-permute-start.24 = (bf16[8,8192]{1,0:T(8,128)(2,1)S(1)}, bf16[8,8192]{1,0:T(8,128)(2,1)S(1)}, u32[]{:S(2)}, u32[]{:S(2)}) collective-permute-start(bf16[8,8192]{1,0:T(8,128)(2,1)S(1)} %get-tuple-element.54), channel_id=1, source_target_pairs={{0,14},{1,15},{4,10},{5,11},{8,6},{9,7},{12,2},{13,3},{14,0},{15,1... | collective-permute-start | bytes 393224 | tf_op jit(solution)/shard_map/ppermute | solution.py:511
  77.9 4.5 %collective-permute-start.22 = (bf16[8,8192]{1,0:T(8,128)(2,1)S(1)}, bf16[8,8192]{1,0:T(8,128)(2,1)S(1)}, u32[]{:S(2)}, u32[]{:S(2)}) collective-permute-start(bf16[8,8192]{1,0:T(8,128)(2,1)S(1)} %get-tuple-element.52), channel_id=1, source_target_pairs={{0,4},{1,5},{4,8},{5,9},{8,12},{9,13},{12,14},{13,15},{14,10},{15,... | collective-permute-start | bytes 393224 | tf_op jit(solution)/shard_map/ppermute | solution.py:508
  82.5 2.3 %collective-permute-done.22.refs_4_ = bf16[8,8192]{1,0:T(8,128)(2,1)S(1)} collective-permute-done((bf16[8,8192]{1,0:T(8,128)(2,1)S(1)}, bf16[8,8192]{1,0:T(8,128)(2,1)S(1)}, u32[]{:S(2)}, u32[]{:S(2)}) %collective-permute-start.22) | collective-permute-done | bytes 131104 | tf_op jit(solution)/shard_map/ppermute | solution.py:508
  84.9 2.4 %collective-permute-done.23.refs_5_ = bf16[8,8192]{1,0:T(8,128)(2,1)S(1)} collective-permute-done((bf16[8,8192]{1,0:T(8,128)(2,1)S(1)}, bf16[8,8192]{1,0:T(8,128)(2,1)S(1)}, u32[]{:S(2)}, u32[]{:S(2)}) %collective-permute-start.23) | collective-permute-done | bytes 131104 | tf_op jit(solution)/shard_map/ppermute | solution.py:509
  (63 shorter events, 17.4 us)
Async XLA Ops:
  3.6 6.7 %collective-permute-start.1 = (bf16[16,4096]{1,0:T(8,128)(2,1)S(1)}, bf16[16,4096]{1,0:T(8,128)(2,1)S(1)}, u32[]{:S(2)}, u32[]{:S(2)}) collective-permute-start(bf16[16,4096]{1,0:T(8,128)(2,1)S(1)} %pad_maximum_fusion.refs_0_), channel_id=1, source_target_pairs={{0,4},{1,5},{4,8},{5,9},{8,12},{9,13},{12,14},{13,15},{14,10},{15,... | collective-permute-start | bytes 393224 | tf_op jit(solution)/shard_map/ppermute | solution.py:461
  10.3 20.1 %collective-permute-start.8 = (bf16[2,1024,1024]{2,1,0:T(8,128)(2,1)}, bf16[2,1024,1024]{2,1,0:T(8,128)(2,1)}, u32[]{:S(2)}, u32[]{:S(2)}) collective-permute-start(bf16[2,1024,1024]{2,1,0:T(8,128)(2,1)} %source), channel_id=1, source_target_pairs={{0,1},{1,0},{2,3},{3,2},{4,5},{5,4},{6,7},{7,6},{8,9},{9,8},{10,11... | collective-permute-start | bytes 12582920 | tf_op jit(solution)/shard_map/ppermute | solution.py:466
  10.4 7.1 %collective-permute-start.2 = (bf16[16,4096]{1,0:T(8,128)(2,1)S(1)}, bf16[16,4096]{1,0:T(8,128)(2,1)S(1)}, u32[]{:S(2)}, u32[]{:S(2)}) collective-permute-start(bf16[16,4096]{1,0:T(8,128)(2,1)S(1)} %pad_maximum_fusion.refs_0_), channel_id=1, source_target_pairs={{0,2},{1,3},{4,0},{5,1},{8,4},{9,5},{12,8},{13,9},{14,12},{15,13},... | collective-permute-start | bytes 393224 | tf_op jit(solution)/shard_map/ppermute | solution.py:462
  12.1 16.1 %collective-permute-start.7 = (bf16[16,4096]{1,0:T(8,128)(2,1)S(1)}, bf16[16,4096]{1,0:T(8,128)(2,1)S(1)}, u32[]{:S(2)}, u32[]{:S(2)}) collective-permute-start(bf16[16,4096]{1,0:T(8,128)(2,1)S(1)} %pad_maximum_fusion.refs_0_), channel_id=1, source_target_pairs={{0,14},{1,15},{4,10},{5,11},{8,6},{9,7},{12,2},{13,3},{14,0},{15,1... | collective-permute-start | bytes 393224 | tf_op jit(solution)/shard_map/ppermute | solution.py:464
  16.8 6.5 %collective-permute-start.3 = (bf16[16,4096]{1,0:T(8,128)(2,1)S(1)}, bf16[16,4096]{1,0:T(8,128)(2,1)S(1)}, u32[]{:S(2)}, u32[]{:S(2)}) collective-permute-start(bf16[16,4096]{1,0:T(8,128)(2,1)S(1)} %collective-permute-done.1.refs_1_), channel_id=1, source_target_pairs={{0,4},{1,5},{4,8},{5,9},{8,12},{9,13},{12,14},{13,15},{14,10},{15,... | collective-permute-start | bytes 393224 | tf_op jit(solution)/shard_map/ppermute | solution.py:461
  17.5 7.6 %collective-permute-start.4 = (bf16[16,4096]{1,0:T(8,128)(2,1)S(1)}, bf16[16,4096]{1,0:T(8,128)(2,1)S(1)}, u32[]{:S(2)}, u32[]{:S(2)}) collective-permute-start(bf16[16,4096]{1,0:T(8,128)(2,1)S(1)} %collective-permute-done.2.refs_2_), channel_id=1, source_target_pairs={{0,2},{1,3},{4,0},{5,1},{8,4},{9,5},{12,8},{13,9},{14,12},{15,13},... | collective-permute-start | bytes 393224 | tf_op jit(solution)/shard_map/ppermute | solution.py:462
  23.3 5.2 %collective-permute-start.5 = (bf16[16,4096]{1,0:T(8,128)(2,1)S(1)}, bf16[16,4096]{1,0:T(8,128)(2,1)S(1)}, u32[]{:S(2)}, u32[]{:S(2)}) collective-permute-start(bf16[16,4096]{1,0:T(8,128)(2,1)S(1)} %collective-permute-done.3.refs_3_), channel_id=1, source_target_pairs={{0,4},{1,5},{4,8},{5,9},{8,12},{9,13},{12,14},{13,15},{14,10},{15,... | collective-permute-start | bytes 393224 | tf_op jit(solution)/shard_map/ppermute | solution.py:461
  25.0 5.4 %collective-permute-start.6 = (bf16[16,4096]{1,0:T(8,128)(2,1)S(1)}, bf16[16,4096]{1,0:T(8,128)(2,1)S(1)}, u32[]{:S(2)}, u32[]{:S(2)}) collective-permute-start(bf16[16,4096]{1,0:T(8,128)(2,1)S(1)} %collective-permute-done.4.refs_4_), channel_id=1, source_target_pairs={{0,2},{1,3},{4,0},{5,1},{8,4},{9,5},{12,8},{13,9},{14,12},{15,13},... | collective-permute-start | bytes 393224 | tf_op jit(solution)/shard_map/ppermute | solution.py:462
  37.1 10.5 %collective-permute-start.10 = (bf16[528,128]{1,0:T(8,128)(2,1)S(1)}, bf16[528,128]{1,0:T(8,128)(2,1)S(1)}, u32[]{:S(2)}, u32[]{:S(2)}) collective-permute-start(bf16[528,128]{1,0:T(8,128)(2,1)S(1)} %get-tuple-element.37), channel_id=1, source_target_pairs={{0,2},{1,3},{4,0},{5,1},{8,4},{9,5},{12,8},{13,9},{14,12},{15,13},... | collective-permute-start | bytes 405512 | tf_op jit(solution)/shard_map/ppermute | solution.py:493
  37.8 9.8 %collective-permute-start.9 = (bf16[528,128]{1,0:T(8,128)(2,1)S(1)}, bf16[528,128]{1,0:T(8,128)(2,1)S(1)}, u32[]{:S(2)}, u32[]{:S(2)}) collective-permute-start(bf16[528,128]{1,0:T(8,128)(2,1)S(1)} %get-tuple-element.35), channel_id=1, source_target_pairs={{0,4},{1,5},{4,8},{5,9},{8,12},{9,13},{12,14},{13,15},{14,10},{15,... | collective-permute-start | bytes 405512 | tf_op jit(solution)/shard_map/ppermute | solution.py:492
  39.2 21.9 %collective-permute-start.15 = (bf16[528,128]{1,0:T(8,128)(2,1)S(1)}, bf16[528,128]{1,0:T(8,128)(2,1)S(1)}, u32[]{:S(2)}, u32[]{:S(2)}) collective-permute-start(bf16[528,128]{1,0:T(8,128)(2,1)S(1)} %get-tuple-element.43), channel_id=1, source_target_pairs={{0,14},{1,15},{4,10},{5,11},{8,6},{9,7},{12,2},{13,3},{14,0},{15,1... | collective-permute-start | bytes 405512 | tf_op jit(solution)/shard_map/ppermute | solution.py:495
  47.8 7.3 %collective-permute-start.11 = (bf16[528,128]{1,0:T(8,128)(2,1)S(1)}, bf16[528,128]{1,0:T(8,128)(2,1)S(1)}, u32[]{:S(2)}, u32[]{:S(2)}) collective-permute-start(bf16[528,128]{1,0:T(8,128)(2,1)S(1)} %get-tuple-element.38), channel_id=1, source_target_pairs={{0,4},{1,5},{4,8},{5,9},{8,12},{9,13},{12,14},{13,15},{14,10},{15,... | collective-permute-start | bytes 405512 | tf_op jit(solution)/shard_map/ppermute | solution.py:492
  48.3 6.8 %collective-permute-start.12 = (bf16[528,128]{1,0:T(8,128)(2,1)S(1)}, bf16[528,128]{1,0:T(8,128)(2,1)S(1)}, u32[]{:S(2)}, u32[]{:S(2)}) collective-permute-start(bf16[528,128]{1,0:T(8,128)(2,1)S(1)} %get-tuple-element.40), channel_id=1, source_target_pairs={{0,2},{1,3},{4,0},{5,1},{8,4},{9,5},{12,8},{13,9},{14,12},{15,13},... | collective-permute-start | bytes 405512 | tf_op jit(solution)/shard_map/ppermute | solution.py:493
  55.2 6.0 %collective-permute-start.13 = (bf16[528,128]{1,0:T(8,128)(2,1)S(1)}, bf16[528,128]{1,0:T(8,128)(2,1)S(1)}, u32[]{:S(2)}, u32[]{:S(2)}) collective-permute-start(bf16[528,128]{1,0:T(8,128)(2,1)S(1)} %get-tuple-element.41), channel_id=1, source_target_pairs={{0,4},{1,5},{4,8},{5,9},{8,12},{9,13},{12,14},{13,15},{14,10},{15,... | collective-permute-start | bytes 405512 | tf_op jit(solution)/shard_map/ppermute | solution.py:492
  55.8 5.4 %collective-permute-start.14 = (bf16[528,128]{1,0:T(8,128)(2,1)S(1)}, bf16[528,128]{1,0:T(8,128)(2,1)S(1)}, u32[]{:S(2)}, u32[]{:S(2)}) collective-permute-start(bf16[528,128]{1,0:T(8,128)(2,1)S(1)} %get-tuple-element.42), channel_id=1, source_target_pairs={{0,2},{1,3},{4,0},{5,1},{8,4},{9,5},{12,8},{13,9},{14,12},{15,13},... | collective-permute-start | bytes 405512 | tf_op jit(solution)/shard_map/ppermute | solution.py:493
  62.9 2.0 %collective-permute-start.16 = (bf16[8,8,4096]{2,1,0:T(8,128)(2,1)S(1)}, bf16[8,8,4096]{2,1,0:T(8,128)(2,1)S(1)}, u32[]{:S(2)}, u32[]{:S(2)}) collective-permute-start(bf16[8,8,4096]{2,1,0:T(8,128)(2,1)S(1)} %get-tuple-element.45), channel_id=1, source_target_pairs={{0,1},{1,0},{2,3},{3,2},{4,5},{5,4},{6,7},{7,6},{8,9},{9,8},{10,11... | collective-permute-start | bytes 1572872 | tf_op jit(solution)/shard_map/ppermute | solution.py:503
  63.0 2.6 %collective-permute-start.17 = (bf16[8,8,4096]{2,1,0:T(8,128)(2,1)S(1)}, bf16[8,8,4096]{2,1,0:T(8,128)(2,1)S(1)}, u32[]{:S(2)}, u32[]{:S(2)}) collective-permute-start(bf16[8,8,4096]{2,1,0:T(8,128)(2,1)S(1)} %get-tuple-element.47), channel_id=1, source_target_pairs={{0,1},{1,0},{2,3},{3,2},{4,5},{5,4},{6,7},{7,6},{8,9},{9,8},{10,11... | collective-permute-start | bytes 1572872 | tf_op jit(solution)/shard_map/ppermute | solution.py:503
  65.7 5.6 %collective-permute-start.18 = (bf16[8,8192]{1,0:T(8,128)(2,1)S(1)}, bf16[8,8192]{1,0:T(8,128)(2,1)S(1)}, u32[]{:S(2)}, u32[]{:S(2)}) collective-permute-start(bf16[8,8192]{1,0:T(8,128)(2,1)S(1)} %get-tuple-element.48), channel_id=1, source_target_pairs={{0,4},{1,5},{4,8},{5,9},{8,12},{9,13},{12,14},{13,15},{14,10},{15,... | collective-permute-start | bytes 393224 | tf_op jit(solution)/shard_map/ppermute | solution.py:508
  66.3 5.3 %collective-permute-start.19 = (bf16[8,8192]{1,0:T(8,128)(2,1)S(1)}, bf16[8,8192]{1,0:T(8,128)(2,1)S(1)}, u32[]{:S(2)}, u32[]{:S(2)}) collective-permute-start(bf16[8,8192]{1,0:T(8,128)(2,1)S(1)} %get-tuple-element.49), channel_id=1, source_target_pairs={{0,2},{1,3},{4,0},{5,1},{8,4},{9,5},{12,8},{13,9},{14,12},{15,13},... | collective-permute-start | bytes 393224 | tf_op jit(solution)/shard_map/ppermute | solution.py:509
  71.6 5.0 %collective-permute-start.20 = (bf16[8,8192]{1,0:T(8,128)(2,1)S(1)}, bf16[8,8192]{1,0:T(8,128)(2,1)S(1)}, u32[]{:S(2)}, u32[]{:S(2)}) collective-permute-start(bf16[8,8192]{1,0:T(8,128)(2,1)S(1)} %get-tuple-element.50), channel_id=1, source_target_pairs={{0,4},{1,5},{4,8},{5,9},{8,12},{9,13},{12,14},{13,15},{14,10},{15,... | collective-permute-start | bytes 393224 | tf_op jit(solution)/shard_map/ppermute | solution.py:508
  72.7 5.1 %collective-permute-start.21 = (bf16[8,8192]{1,0:T(8,128)(2,1)S(1)}, bf16[8,8192]{1,0:T(8,128)(2,1)S(1)}, u32[]{:S(2)}, u32[]{:S(2)}) collective-permute-start(bf16[8,8192]{1,0:T(8,128)(2,1)S(1)} %get-tuple-element.51), channel_id=1, source_target_pairs={{0,2},{1,3},{4,0},{5,1},{8,4},{9,5},{12,8},{13,9},{14,12},{15,13},... | collective-permute-start | bytes 393224 | tf_op jit(solution)/shard_map/ppermute | solution.py:509
  73.7 8.8 %collective-permute-start.24 = (bf16[8,8192]{1,0:T(8,128)(2,1)S(1)}, bf16[8,8192]{1,0:T(8,128)(2,1)S(1)}, u32[]{:S(2)}, u32[]{:S(2)}) collective-permute-start(bf16[8,8192]{1,0:T(8,128)(2,1)S(1)} %get-tuple-element.54), channel_id=1, source_target_pairs={{0,14},{1,15},{4,10},{5,11},{8,6},{9,7},{12,2},{13,3},{14,0},{15,1... | collective-permute-start | bytes 393224 | tf_op jit(solution)/shard_map/ppermute | solution.py:511
  77.9 7.0 %collective-permute-start.22 = (bf16[8,8192]{1,0:T(8,128)(2,1)S(1)}, bf16[8,8192]{1,0:T(8,128)(2,1)S(1)}, u32[]{:S(2)}, u32[]{:S(2)}) collective-permute-start(bf16[8,8192]{1,0:T(8,128)(2,1)S(1)} %get-tuple-element.52), channel_id=1, source_target_pairs={{0,4},{1,5},{4,8},{5,9},{8,12},{9,13},{12,14},{13,15},{14,10},{15,... | collective-permute-start | bytes 393224 | tf_op jit(solution)/shard_map/ppermute | solution.py:508
  82.4 5.0 %collective-permute-start.23 = (bf16[8,8192]{1,0:T(8,128)(2,1)S(1)}, bf16[8,8192]{1,0:T(8,128)(2,1)S(1)}, u32[]{:S(2)}, u32[]{:S(2)}) collective-permute-start(bf16[8,8192]{1,0:T(8,128)(2,1)S(1)} %get-tuple-element.53), channel_id=1, source_target_pairs={{0,2},{1,3},{4,0},{5,1},{8,4},{9,5},{12,8},{13,9},{14,12},{15,13},... | collective-permute-start | bytes 393224 | tf_op jit(solution)/shard_map/ppermute | solution.py:509
  (5 other events, 37.0 us)
